TPU v7x, 256 devices: a whole 4x4x8 slice. The times are simulated.
256 devices in a mesh: seq: 32 (over z, y), head: 8 (over x, core).
Axes of the slice: x: 4, y: 4, z: 8, core: 2. Of those that a mesh axis runs over, the one named last changes fastest.
Arguments:
- queries: bfloat16 [4096, 8192], P('seq', 'head'), may hold values from -6 to 6
- key_vectors: bfloat16 [4096, 8192], P('seq', 'head'), may hold values from -6 to 6
- value_vectors: bfloat16 [4096, 8192], P('seq', 'head'), may hold values from -6 to 6
- log_decay: float32 [4096, 64], P('seq', 'head'), may hold values from -2 to 0
- doc_ids: int32 [4096], P('seq'), may hold values from 0 to 3, as said below
- head_gain: float32 [8192], P('head'), may hold values from 0.4 to 1.6
- output_weight: bfloat16 [8192, 3072], P('head', 'seq'), may hold values from -0.0625 to 0.0625
- residual: bfloat16 [4096, 3072], P('seq', 'head'), may hold values from -8 to 8
- norm_gain: float32 [3072], replicated, may hold values from 0.4 to 1.6
- routing: int32 [4096, 2], P('seq'), may hold values from 0 to 31, all different within a row; in each aligned block of 128 rows (0 to 127, 128 to 255, ...) at most 16 rows name the same one
- route_weights: float32 [4096, 2], P('seq'), may hold values from 0.1 to 1
- gate_weight: bfloat16 [32, 3072, 4608], P('seq', None, 'head'), may hold values from -0.109375 to 0.109375
- up_weight: bfloat16 [32, 3072, 4608], P('seq', None, 'head'), may hold values from -0.109375 to 0.109375
- down_weight: bfloat16 [32, 4608, 3072], P('seq', 'head'), may hold values from -0.09375 to 0.09375
Outputs:
- mixed: bfloat16 [4096, 3072], P('seq', 'head')
Inputs may be any that keep to these rules, and one draw needn't show every extreme that they name: `doc_ids`: ids never fall along the sequence and rise by one where a document starts; every id occurs. `routing`: the two experts of a position differ; among the rows of one index of seq no expert is named more than 16 times.
All inputs are finite; a program needn't handle non-finite values.
Results may differ from a plain program's by a relative error of at most 0.014.
Values may be sent and summed in bfloat16 or wider, within the bound.
A program may use at most 128 MiB of HBM per device.

v0:
```python
import jax
import jax.numpy as jnp
from jax import lax
from jax.sharding import Mesh
from jax.sharding import PartitionSpec as P

SEQ = ("seq_0", "seq_1")


EPSILON = 1e-06
FULL_PRECISION = lax.Precision.HIGHEST


def nothing_yet(array, identity):
    return jax.tree.map(
        lambda part, zero: jnp.zeros_like(part) + jnp.asarray(zero, part.dtype), array, identity
    )


def collected_together(array, axis):
    leaves = jax.tree.leaves(array)
    sequence = sorted(range(len(leaves)), key=lambda k: -leaves[k].size)
    width = (1, *leaves[sequence[0]].shape)[-1]
    lines = [
        jnp.pad(leaves[k].reshape(-1), (0, -leaves[k].size % width)).reshape(-1, width)
        for k in sequence
    ]
    both, at, found = (lax.all_gather(jnp.concatenate(lines), axis), 0, {})
    for k, line in zip(sequence, lines):
        slab = both[:, at : at + len(line)].reshape(len(both), -1)
        found[k] = slab[:, : leaves[k].size].reshape(-1, *leaves[k].shape)
        at += len(line)
    numbers = iter(range(len(leaves)))
    return jax.tree.map(lambda _: found[next(numbers)], array)


def entering(array, axes, combine, identity):
    before = start = nothing_yet(array, identity)
    running = array
    for axis in reversed(axes):
        size, place = (lax.axis_size(axis), lax.axis_index(axis))
        pieces = collected_together(running, axis)
        inside, running = (start, start)
        for k in range(size):
            passed = k < place
            running = combine(running, jax.tree.map(lambda part: part[k], pieces))
            inside = jax.tree.map(lambda new, old: jnp.where(passed, new, old), running, inside)
        before = combine(inside, before)
    return before


def gather_axes(array, axes, dim):
    filled = array
    for number in range(len(axes) - 1, -1, -1):
        filled = lax.all_gather(filled, axes[number], axis=dim, tiled=True)
    return filled


def in_blocks(array, dim, size):
    before, after = (array.shape[:dim], array.shape[dim + 1 :])
    return jnp.moveaxis(array.reshape(*before, size, -1, *after), dim, 0)


def sum_at_owner(array, axis, dim):
    size = lax.axis_size(axis)
    pieces = lax.all_to_all(in_blocks(array, dim, size), axis, 0, 0, tiled=True)
    return jnp.sum(pieces.astype(jnp.float32), axis=0)


def link_summaries(earlier, later):
    gain_early, state_early, first_early, last_early = earlier
    gain_late, state_late, first_late, last_late = later
    joined = (first_late == last_early) | (last_early < 0.0) | (first_late < 0.0)
    through = gain_late * joined.astype(jnp.float32)
    return (
        gain_early * through,
        through[:, None, None] * state_early + state_late,
        jnp.where(first_early < 0.0, first_late, first_early),
        jnp.where(last_late < 0.0, last_early, last_late),
    )


def shards(
    queries,
    key_vectors,
    value_vectors,
    log_decay,
    doc_ids,
    head_gain,
    output_weight,
    residual,
    norm_gain,
    routing,
    route_weights,
    gate_weight,
    up_weight,
    down_weight,
):
    tokens, heads = log_decay.shape
    head_width = queries.shape[1] // heads
    query_heads = queries.reshape(tokens, heads, head_width)
    key_heads = key_vectors.reshape(tokens, heads, head_width)
    value_heads = value_vectors.reshape(tokens, heads, head_width)
    decay_sum = jnp.cumsum(log_decay, axis=0)
    decay_rows = decay_sum.T
    gap_matrix = decay_rows[:, :, None] - decay_rows[:, None, :]
    row_index = lax.broadcasted_iota(jnp.int32, (tokens, tokens), 0)
    col_index = lax.broadcasted_iota(jnp.int32, (tokens, tokens), 1)
    kept_mask = (col_index <= row_index) & (doc_ids[:, None] == doc_ids[None, :])
    decay_matrix = jnp.where(kept_mask[None], jnp.exp(jnp.minimum(gap_matrix, 0.0)), 0.0)
    scores = jnp.einsum("thd,shd->hts", query_heads, key_heads, preferred_element_type=jnp.float32)
    weighted = (scores * decay_matrix).astype(jnp.bfloat16)
    inside = jnp.einsum("hts,shd->thd", weighted, value_heads, preferred_element_type=jnp.float32)
    doc_float = doc_ids.astype(jnp.float32)
    tail_gain = (
        jnp.exp(decay_sum[-1][None, :] - decay_sum)
        * (doc_ids == doc_ids[-1]).astype(jnp.float32)[:, None]
    )
    own_state = jnp.einsum(
        "thd,the->hde",
        key_heads.astype(jnp.float32) * tail_gain[:, :, None],
        value_heads.astype(jnp.float32),
        precision=FULL_PRECISION,
    )
    own_gain = jnp.exp(decay_sum[-1]) * (doc_ids[0] == doc_ids[-1]).astype(jnp.float32)
    summary = (own_gain, own_state, doc_float[:1], doc_float[-1:])
    identity = (
        jnp.ones((heads,), jnp.float32),
        jnp.zeros_like(own_state),
        jnp.full((1,), -1.0, jnp.float32),
        jnp.full((1,), -1.0, jnp.float32),
    )
    _, entered, _, before = entering(summary, SEQ, link_summaries, identity)
    reach_gain = jnp.exp(decay_sum) * (doc_float == before[0]).astype(jnp.float32)[:, None]
    outside = (
        jnp.einsum(
            "thd,hde->the", query_heads.astype(jnp.float32), entered, precision=FULL_PRECISION
        )
        * reach_gain[:, :, None]
    )
    heads_raw = inside + outside
    inv_norm = lax.rsqrt(jnp.mean(heads_raw * heads_raw, axis=2, keepdims=True) + EPSILON)
    attended = ((heads_raw * inv_norm).reshape(tokens, heads * head_width) * head_gain).astype(
        jnp.bfloat16
    )
    partial_value = jnp.dot(
        attended, gather_axes(output_weight, SEQ, 1), preferred_element_type=jnp.float32
    )
    model_width = partial_value.shape[1]
    head_count = lax.axis_size("head")
    part_width = model_width // head_count
    offset = lax.axis_index("head") * part_width
    summed = sum_at_owner(partial_value.astype(jnp.bfloat16), "head", 1)
    middle = lax.optimization_barrier((summed + residual.astype(jnp.float32)).astype(jnp.bfloat16))
    middle_float = middle.astype(jnp.float32)
    squares = lax.psum(jnp.sum(middle_float * middle_float, axis=1), "head")
    row_norm = lax.rsqrt(squares / model_width + EPSILON)[:, None]
    gain_part = lax.dynamic_slice_in_dim(norm_gain, offset, part_width, 0)
    normed_part = (middle_float * row_norm * gain_part).astype(jnp.bfloat16)
    experts = lax.axis_size(SEQ)
    capacity = 4 * tokens // experts
    flat_ids = routing.reshape(-1)
    hit_table = (flat_ids[:, None] == jnp.arange(experts, dtype=jnp.int32)[None, :]).astype(
        jnp.int32
    )
    slot_rank = jnp.sum((jnp.cumsum(hit_table, axis=0) - 1) * hit_table, axis=1)
    slot_place = flat_ids * capacity + slot_rank
    owner_row = jnp.arange(2 * tokens, dtype=jnp.int32) // 2
    slot_table = jnp.full((experts * capacity,), tokens, jnp.int32).at[slot_place].set(owner_row)
    mix_weights = route_weights.reshape(-1)[:, None]
    gate_local = gate_weight[0]
    up_local = up_weight[0]
    down_local = down_weight[0]
    padded = jnp.concatenate([normed_part, jnp.zeros((1, part_width), jnp.bfloat16)], axis=0)
    outgoing = padded[slot_table].reshape(experts, capacity, part_width)
    gathered = lax.all_gather(
        lax.all_to_all(outgoing, SEQ, split_axis=0, concat_axis=0, tiled=True),
        "head",
        axis=2,
        tiled=True,
    )
    sources = gathered.shape[0]
    slot_count = gathered.shape[1]
    row_block = gathered.reshape(sources * slot_count, model_width)
    gate_proj = jnp.dot(row_block, gate_local, preferred_element_type=jnp.float32)
    up_proj = jnp.dot(row_block, up_local, preferred_element_type=jnp.float32)
    hidden = (jax.nn.silu(gate_proj) * up_proj).astype(jnp.bfloat16)
    result = (
        jnp.dot(hidden, down_local, preferred_element_type=jnp.float32)
        .astype(jnp.bfloat16)
        .astype(jnp.float32)
    )
    summed_out = sum_at_owner(
        result.reshape(sources, slot_count, model_width).astype(jnp.bfloat16), "head", 2
    )
    returned = lax.all_to_all(
        summed_out.astype(jnp.bfloat16), SEQ, split_axis=0, concat_axis=0, tiled=True
    ).astype(summed_out.dtype)
    picked = returned.reshape(-1, part_width)[slot_place] * mix_weights
    expert_sum = jnp.sum(picked.reshape(tokens, 2, part_width), axis=1)
    return (middle_float + expert_sum).astype(jnp.bfloat16)


def solution(mesh):
    torus = Mesh(mesh.devices.reshape(8, 4, mesh.shape["head"]), ("seq_0", "seq_1", "head"))
    in_specs = (
        P(SEQ, "head"),
        P(SEQ, "head"),
        P(SEQ, "head"),
        P(SEQ, "head"),
        P(SEQ),
        P("head"),
        P("head", SEQ),
        P(SEQ, "head"),
        P(),
        P(SEQ, None),
        P(SEQ, None),
        P(SEQ, None, "head"),
        P(SEQ, None, "head"),
        P(SEQ, "head", None),
    )
    out_specs = P(SEQ, "head")
    return jax.shard_map(
        shards, mesh=torus, in_specs=in_specs, out_specs=out_specs, check_vma=False
    )
```

profile of v0, /device:TPU:2, one launch (start us, length us, event | category | flops | bytes accessed | tf_op | source)
XLA Modules:
  0.0 410.7 jit_solution(2517632660121029488)
XLA Ops:
  8.6 1.8 copy.85
  13.1 1.6 reduce_window_sum.24
  21.7 2.2 fusion.57
  23.9 2.4 concatenate.9
  26.3 36.5 %all-gather.13.cloned.1.call-done = f32[4,1027,128]{2,1,0:T(8,128)} async-done(((f32[1,1027,128]{2,1,0:T(8,128)}), f32[4,1027,128]{2,1,0:T(8,128)}) %all-gather.13.cloned.1.call-update) | async-done | bytes 2103312 | tf_op jit(solution)/shard_map/all_gather | solution.py:28
  79.0 2.8 bitcast_add_fusion
  81.8 3.0 concatenate.10
  84.9 14.3 %all_gather.25 = bf16[1024,384]{0,1:T(8,128)(2,1)} all-gather(bf16[1024,96]{0,1:T(8,128)(2,1)} %param.20), channel_id=1, replica_groups=mesh['seq_0'=8,'seq_1'=4,'head'=8] {'seq_1'}, dimensions={1}, use_global_device_ids=true | all-gather | bytes 983040 | tf_op jit(solution)/shard_map/all_gather | solution.py:55
  103.1 1.9 reduce-window.6
  109.0 2.9 fusion.124
  111.9 28.2 %all-gather.15.cloned.1.call-done = f32[8,1027,128]{2,1,0:T(8,128)} async-done(((f32[1,1027,128]{2,1,0:T(8,128)}), f32[8,1027,128]{2,1,0:T(8,128)}) %all-gather.15.cloned.1.call-update) | async-done | bytes 4206608 | tf_op jit(solution)/shard_map/all_gather | solution.py:28
  163.7 2.6 fusion.122
  166.5 2.1 fusion.12
  168.6 2.6 multiply_reduce_fusion
  173.9 41.0 %all-gather.9.cloned.1.call-done = bf16[1024,3072]{0,1:T(8,128)(2,1)} async-done(((bf16[1024,384]{0,1:T(8,128)(2,1)}), bf16[1024,3072]{0,1:T(8,128)(2,1)}) %all-gather.9.cloned.1.call-update) | async-done | bytes 6291472 | tf_op jit(solution)/shard_map/all_gather | solution.py:55
  215.0 5.1 %convolution_convert_fusion.1 = bf16[128,3072]{1,0:T(8,128)(2,1)S(1)} fusion(bf16[128,1024]{0,1:T(8,128)(2,1)} %fusion.17, bf16[1024,3072]{0,1:T(8,128)(2,1)} %all-gather.9.cloned.1.call-done), kind=kOutput, calls=%fused_computation.4 | convolution fusion | flops 805699584 | bytes 7340032 | tf_op jit(solution)/shard_map/dot_general | solution.py:146
  221.1 4.8 %all-to-all-start = ((bf16[8,128,384]{2,1,0:T(8,128)(2,1)}), bf16[8,128,384]{2,1,0:T(8,128)(2,1)}, u32[]{:S(2)}, u32[]{:S(2)}) async-start(bf16[8,128,384]{2,1,0:T(8,128)(2,1)} %bitcast.254), calls=%async_computation | async-start | bytes 1572864 | tf_op jit(solution)/shard_map/all_to_all | solution.py:66
  233.0 4.6 %all-to-all-done = bf16[8,128,384]{2,1,0:T(8,128)(2,1)} async-done(((bf16[8,128,384]{2,1,0:T(8,128)(2,1)}), bf16[8,128,384]{2,1,0:T(8,128)(2,1)}, u32[]{:S(2)}, u32[]{:S(2)}) %all-to-all-start) | async-done | bytes 786464 | tf_op jit(solution)/shard_map/all_to_all | solution.py:66
  240.6 11.2 %psum.7 = f32[128]{0:T(128)} all-reduce(f32[128]{0:T(128)S(1)} %fusion.105), channel_id=1, replica_groups=mesh['seq_0'=8,'seq_1'=4,'head'=8] {'head'}, use_global_device_ids=true, to_apply=%region_4.5 | all-reduce | flops 128 | bytes 1024 | tf_op jit(solution)/shard_map/psum | solution.py:156
  254.0 3.4 gather_fusion
  257.4 22.4 %all_to_all.20 = bf16[32,16,384]{2,1,0:T(8,128)(2,1)} all-to-all(bf16[32,16,384]{2,1,0:T(8,128)(2,1)} %bitcast.270), channel_id=1, replica_groups=mesh['seq_0'=8,'seq_1'=4,'head'=8] {'seq_0','seq_1'}, dimensions={0} | all-to-all | bytes 786432 | tf_op jit(solution)/shard_map/all_to_all | solution.py:177
  279.8 25.7 %all-gather.11.cloned.1.call-done = bf16[32,16,3072]{2,1,0:T(8,128)(2,1)} async-done(((bf16[32,16,384]{2,1,0:T(8,128)(2,1)}), bf16[32,16,3072]{2,1,0:T(8,128)(2,1)}) %all-gather.11.cloned.1.call-update) | async-done | bytes 3145744 | tf_op jit(solution)/shard_map/all_gather | solution.py:176
  305.5 6.0 %fusion.3 = f32[512,576]{0,1:T(8,128)} fusion(bf16[512,3072]{1,0:T(8,128)(2,1)} %bitcast.284, bf16[1,3072,576]{1,2,0:T(8,128)(2,1)} %param.25), kind=kOutput, calls=%fused_computation.8 | convolution fusion | flops 1811939328 | bytes 7864320 | tf_op jit(solution)/shard_map/dot_general | solution.py:185
  311.5 9.5 %convolution_convert_fusion = bf16[512,3072]{1,0:T(8,128)(2,1)} fusion(bf16[1,576,3072]{2,1,0:T(8,128)(2,1)S(1)} %copy-done, bf16[512,3072]{1,0:T(8,128)(2,1)} %bitcast.285, bf16[1,3072,576]{1,2,0:T(8,128)(2,1)} %param.26, f32[512,576]{0,1:T(8,128)} %fusion.3), kind=kOutput, calls=%fused_computation.3 | convolution fusion | flops 3627220992 | bytes 14548992 | tf_op jit(solution)/shard_map/dot_general | solution.py:189
  321.0 2.6 copy.90
  324.0 41.9 %all_to_all.21 = bf16[8,32,16,384]{3,2,1,0:T(8,128)(2,1)} all-to-all(bf16[8,32,16,384]{3,2,1,0:T(8,128)(2,1)S(1)} %bitcast.251), channel_id=1, replica_groups=mesh['seq_0'=8,'seq_1'=4,'head'=8] {'head'}, dimensions={0} | all-to-all | bytes 6291456 | tf_op jit(solution)/shard_map/all_to_all | solution.py:66
  366.0 3.2 reduce_sum.64
  369.2 10.0 %all-to-all-start.3 = ((bf16[32,16,384]{2,1,0:T(8,128)(2,1)}), bf16[32,16,384]{2,1,0:T(8,128)(2,1)}, u32[]{:S(2)}, u32[]{:S(2)}) async-start(bf16[32,16,384]{2,1,0:T(8,128)(2,1)} %reduce_sum.64), calls=%async_computation.3 | async-start | bytes 786432 | tf_op jit(solution)/shard_map/all_to_all | solution.py:196
  379.9 14.3 %all-to-all-done.3 = bf16[32,16,384]{2,1,0:T(8,128)(2,1)} async-done(((bf16[32,16,384]{2,1,0:T(8,128)(2,1)}), bf16[32,16,384]{2,1,0:T(8,128)(2,1)}, u32[]{:S(2)}, u32[]{:S(2)}) %all-to-all-start.3) | async-done | bytes 393248 | tf_op jit(solution)/shard_map/all_to_all | solution.py:196
  394.1 1.9 bitcast_convert_fusion
  396.1 3.0 gather_fusion.1
  399.1 2.0 gather.10
  (110 shorter events, 47.5 us)
Async XLA Ops:
  6.5 304.9 %copy-start = (bf16[1,576,3072]{2,1,0:T(8,128)(2,1)S(1)}, bf16[1,576,3072]{2,1,0:T(8,128)(2,1)}, u32[]{:S(2)}) copy-start(bf16[1,576,3072]{2,1,0:T(8,128)(2,1)} %param.27) | copy-start | bytes 10616836
  6.5 56.3 %all-gather.13.cloned.1.call-start = ((), (), s32[]{:S(2)}) async-start(), calls=%async_computation.6 | async-start | bytes 2641920 | tf_op jit(solution)/shard_map/all_gather | solution.py:28
  26.3 74.5 %copy-start.14 = (s32[128,2]{0,1:T(2,128)S(1)}, s32[128,2]{0,1:T(2,128)}, u32[]{:S(2)}) copy-start(s32[128,2]{0,1:T(2,128)} %param.23) | copy-start | bytes 3076
  26.3 113.8 %all-gather.15.cloned.1.call-start = ((), (), s32[]{:S(2)}) async-start(), calls=%async_computation.7 | async-start | bytes 4755456 | tf_op jit(solution)/shard_map/all_gather | solution.py:28
  72.6 5.8 %copy-start.8 = (f32[8]{0:T(128)}, f32[8]{0:T(128)S(1)}, u32[]{:S(2)}) copy-start(f32[8]{0:T(128)S(1)} %get-tuple-element.8) | copy-start | bytes 100
  72.6 5.8 %copy-start.10 = (f32[8]{0:T(128)}, f32[8]{0:T(128)S(1)}, u32[]{:S(2)}) copy-start(f32[8]{0:T(128)S(1)} %get-tuple-element.6) | copy-start | bytes 100
  72.6 5.8 %copy-start.12 = (f32[8]{0:T(128)}, f32[8]{0:T(128)S(1)}, u32[]{:S(2)}) copy-start(f32[8]{0:T(128)S(1)} %get-tuple-element.58) | copy-start | bytes 100
  72.7 5.8 %copy-start.17 = (f32[8]{0:T(128)}, f32[8]{0:T(128)S(1)}, u32[]{:S(2)}) copy-start(f32[8]{0:T(128)S(1)} %get-tuple-element.5) | copy-start | bytes 100
  79.0 28.7 %copy-start.7 = (s32[128]{0:T(128)S(1)}, s32[128]{0:T(128)}, u32[]{:S(2)}) copy-start(s32[128]{0:T(128)} %param.18) | copy-start | bytes 1540
  84.9 130.1 %all-gather.9.cloned.1.call-start = ((), (), s32[]{:S(2)}) async-start(), calls=%async_computation.4 | async-start | bytes 7077888 | tf_op jit(solution)/shard_map/all_gather | solution.py:55
  163.6 2.7 copy-start.1
  163.6 2.7 copy-start.2
  163.6 2.7 copy-start.3
  163.7 2.8 copy-start.4
  163.7 2.9 copy-start.6
  163.7 2.9 copy-start.9
  163.7 2.9 copy-start.11
  163.7 2.8 copy-start.13
  220.1 7.4 %copy-start.15 = (s32[128,2]{0,1:T(2,128)S(1)}, s32[128,2]{0,1:T(2,128)}, u32[]{:S(2)}) copy-start(s32[128,2]{0,1:T(2,128)} %broadcast_multiply_fusion.1) | copy-start | bytes 3076
  220.1 9.1 %copy-start.16 = (s32[32,2]{0,1:T(2,128)S(1)}, s32[32,2]{0,1:T(2,128)}, u32[]{:S(2)}) copy-start(s32[32,2]{0,1:T(2,128)} %slice_reduce_fusion) | copy-start | bytes 772
  221.1 16.6 %all-to-all-start = ((bf16[8,128,384]{2,1,0:T(8,128)(2,1)}), bf16[8,128,384]{2,1,0:T(8,128)(2,1)}, u32[]{:S(2)}, u32[]{:S(2)}) async-start(bf16[8,128,384]{2,1,0:T(8,128)(2,1)} %bitcast.254), calls=%async_computation | async-start | bytes 1572864 | tf_op jit(solution)/shard_map/all_to_all | solution.py:66
  225.9 79.6 %all-gather.11.cloned.1.call-start = ((), (), s32[]{:S(2)}) async-start(), calls=%async_computation.5 | async-start | bytes 3538944 | tf_op jit(solution)/shard_map/all_gather | solution.py:176
  239.8 0.6 copy-start.5
  366.0 13.2 %copy-start.18 = (f32[128,2]{0,1:T(2,128)S(1)}, f32[128,2]{0,1:T(2,128)}, u32[]{:S(2)}) copy-start(f32[128,2]{0,1:T(2,128)} %param.24) | copy-start | bytes 3076
  369.2 25.0 %all-to-all-start.3 = ((bf16[32,16,384]{2,1,0:T(8,128)(2,1)}), bf16[32,16,384]{2,1,0:T(8,128)(2,1)}, u32[]{:S(2)}, u32[]{:S(2)}) async-start(bf16[32,16,384]{2,1,0:T(8,128)(2,1)} %reduce_sum.64), calls=%async_computation.3 | async-start | bytes 786432 | tf_op jit(solution)/shard_map/all_to_all | solution.py:196
Sparse Core Ops, SparseCore 0:
  26.4 36.4 all-gather.12
  85.0 55.0 all-gather.14
  141.9 73.0 all-gather.8
  279.9 25.4 all-gather.10
where the time goes:
time: 413 us; the launch traced here: 411 us
  waiting for transfers between devices  150 us (36%)
  blocking collectives  89.9 us (22%)
  local copies, waits for them, and re-layouts  49.6 us (12%)
  between operations  45.7 us (11%)
  other arithmetic  32.8 us (8%)
  matrix products  27.5 us (7%)
  starting transfers between devices  14.9 us (4%)
    all_gather x2, waiting for transfers between devices, collected_together(): both, at, found = (lax.all_gather(jnp.concatenate(lines), axis), 0, {})  64.7 us
    all_to_all x1, blocking collectives, sum_at_owner(): pieces = lax.all_to_all(in_blocks(array, dim, size), axis, 0, 0, tiled=True)  41.9 us
    all_gather x1, waiting for transfers between devices, gather_axes(): filled = lax.all_gather(filled, axes[number], axis=dim, tiled=True)  41 us
    all_gather x1, waiting for transfers between devices, shards(): lax.all_gather(lax.all_to_all(outgoing, SEQ, split_axis=0, concat_axis=0,...  25.7 us
    all_to_all x1, blocking collectives, shards(): lax.all_to_all(outgoing, SEQ, split_axis=0, concat_axis=0, tiled=True)  22.4 us
    all_gather x1, blocking collectives, gather_axes(): filled = lax.all_gather(filled, axes[number], axis=dim, tiled=True)  14.3 us
    all_to_all x1, waiting for transfers between devices, shards(): lax.all_to_all(summed_out.astype(jnp.bfloat16), SEQ, split_axis=0, concat...  14.3 us
    psum x1, blocking collectives, shards(): squares = lax.psum(jnp.sum(middle_float * middle_float, axis=1), 'head')  11.2 us
  transfers between devices with their start and end apart: 6, of which 6 were waited for; matrix products, arithmetic and copies ran while one was open for 9% of the time, Pallas kernels for 0%

commit v1 on v0

v1 whole, which is shorter than its diff:
```python
import functools

import jax
import jax.numpy as jnp
from jax import lax
from jax.experimental import pallas as pl
from jax.experimental.pallas import tpu as pltpu
from jax.sharding import PartitionSpec as P

MESH = pl.DeviceIdType.MESH
F32, BF16 = jnp.float32, jnp.bfloat16
EPSILON = 1e-06
NZ, NY, NX = 8, 4, 4
NSEQ, NHEAD = NZ * NY, 2 * NX
TOK, HEADS, HD = 128, 8, 128
WCOLS = 96
PART = 384
D = PART * NHEAD
CAP = 16
NG = 4
GSRC = NSEQ // NG
GROWS = GSRC * CAP
FF = 576
VMEM_LIMIT = 60 * 1024 * 1024


def nt(a, b):
    return lax.dot_general(a, b, (((1,), (1,)), ((), ())), preferred_element_type=F32)


def nn(a, b):
    return jnp.dot(a, b, preferred_element_type=F32)


def remote(src, dst, send_sem, recv_sem, **device):
    return pltpu.make_async_remote_copy(
        src_ref=src,
        dst_ref=dst,
        send_sem=send_sem,
        recv_sem=recv_sem,
        device_id=device,
        device_id_type=MESH,
    )


def greet(me, hd):
    barrier = pltpu.get_barrier_semaphore()

    @pl.loop(1, NSEQ)
    def _(d):
        pl.semaphore_signal(
            barrier, inc=1, device_id={"seq": lax.rem(me + d, NSEQ)}, device_id_type=MESH
        )

    @pl.loop(1, NHEAD)
    def _(d):
        pl.semaphore_signal(
            barrier, inc=1, device_id={"head": lax.rem(hd + d, NHEAD)}, device_id_type=MESH
        )

    return barrier


def columns(row):
    return jnp.transpose(jnp.broadcast_to(row, (TOK, TOK)))


def attention_kernel(
    q_ref,
    k_ref,
    v_ref,
    ld_ref,
    doc_ref,
    hg_ref,
    w_ref,
    res_ref,
    mid_ref,
    decay,
    own_state,
    own_info,
    all_state,
    all_info,
    own_carry,
    all_carry,
    inner,
    attended,
    weight,
    partial,
    arrived,
    column_out,
    column_in,
    s_state,
    r_state,
    s_info,
    r_info,
    s_carry,
    r_carry,
    s_att,
    r_att,
    s_w,
    r_w,
    s_part,
    r_part,
    s_col,
    r_col,
):
    me, hd = lax.axis_index("seq"), lax.axis_index("head")
    zi, yi = me // NY, lax.rem(me, NY)
    barrier = greet(me, hd)

    rows = lax.broadcasted_iota(jnp.int32, (TOK, TOK), 0)
    cols = lax.broadcasted_iota(jnp.int32, (TOK, TOK), 1)
    upper = (rows <= cols).astype(F32)
    sums = jnp.dot(
        ld_ref[...], upper, preferred_element_type=F32, precision=lax.Precision.HIGHEST
    )
    decay[...] = sums
    last = sums[:, TOK - 1 : TOK]
    doc = doc_ref[...].astype(F32)
    doc_first, doc_last = doc[:, 0:1], doc[:, TOK - 1 : TOK]
    tail = jnp.exp(last - sums) * (doc == doc_last).astype(F32)
    gain = jnp.exp(last) * (doc_first == doc_last).astype(F32)
    own_info[0:8, :] = jnp.broadcast_to(gain, (HEADS, TOK))
    own_info[8:16, :] = jnp.where(
        lax.broadcasted_iota(jnp.int32, (8, TOK), 0) == 0, doc_first, doc_last
    )
    for h in range(HEADS):
        lanes = slice(h * HD, (h + 1) * HD)
        key_t = jnp.transpose(k_ref[:, lanes].astype(F32))
        state = nn((key_t * tail[h : h + 1, :]).astype(BF16), v_ref[:, lanes])
        own_state[4 * h : 4 * h + 4] = state.astype(BF16).reshape(4, 32, HD)

    pl.semaphore_wait(barrier, NSEQ + NHEAD - 2)

    @pl.loop(1, NSEQ)
    def _(d):
        to = lax.rem(me + d, NSEQ)
        remote(own_info, all_info.at[me], s_info, r_info, seq=to).start()
        remote(own_state.at[to], all_state.at[me], s_state, r_state, seq=to).start()

    all_state[me] = own_state[me]
    all_info[me] = own_info[...]

    w_rows = pl.ds(pl.multiple_of(zi * WCOLS, 32), WCOLS)

    @pl.loop(1, NZ)
    def _(d):
        to = lax.rem(zi + d, NZ) * NY + yi
        remote(w_ref, weight.at[w_rows], s_w, r_w, seq=to).start()

    doc_rows = jnp.broadcast_to(doc, (TOK, TOK))
    kept = (cols <= rows) & (jnp.transpose(doc_rows) == doc_rows)
    for h in range(HEADS):
        lanes = slice(h * HD, (h + 1) * HD)
        decay_row = jnp.broadcast_to(decay[h : h + 1, :], (TOK, TOK))
        gap = jnp.transpose(decay_row) - decay_row
        factor = jnp.where(kept, jnp.exp(jnp.minimum(gap, 0.0)), 0.0)
        weighted = (nt(q_ref[:, lanes], k_ref[:, lanes]) * factor).astype(BF16)
        inner[:, lanes] = nn(weighted, v_ref[:, lanes])
    weight[w_rows, :] = w_ref[...]

    others = NSEQ - 1
    remote(
        own_state.at[0:others], all_state.at[0:others], s_state, r_state, seq=me
    ).wait_recv()
    remote(
        all_info.at[0:others], all_info.at[0:others], s_info, r_info, seq=me
    ).wait_recv()
    my_head = me // 4

    def scan(b, carry):
        carried, before = carry
        own_carry[b] = carried.astype(BF16)
        gain_row = all_info[b, pl.ds(my_head, 1), :]
        docs = all_info[b, 8:16, :]
        through = jnp.where(docs[0:1, :] == before, gain_row, 0.0)
        return all_state[b].astype(F32) + through * carried, docs[1:2, :]

    lax.fori_loop(
        0, NSEQ, scan, (jnp.zeros((32, HD), F32), jnp.full((1, HD), -1.0, F32))
    )

    @pl.loop(1, NSEQ)
    def _(d):
        to = lax.rem(me + d, NSEQ)
        remote(own_carry.at[to], all_carry.at[me], s_carry, r_carry, seq=to).start()

    all_carry[me] = own_carry[me]
    before_doc = all_info[jnp.maximum(me - 1, 0), 8:16, :][1:2, :]
    before_doc = jnp.where(jnp.full((1, TOK), me, jnp.int32) == 0, -1.0, before_doc)
    reach = jnp.exp(decay[...]) * (doc == before_doc).astype(F32)
    remote(
        own_carry.at[0:others], all_carry.at[0:others], s_carry, r_carry, seq=me
    ).wait_recv()
    for h in range(HEADS):
        lanes = slice(h * HD, (h + 1) * HD)
        carried = all_carry[4 * h : 4 * h + 4].reshape(HD, HD)
        raw = inner[:, lanes] + nn(q_ref[:, lanes], carried) * columns(reach[h : h + 1, :])
        scale = lax.rsqrt(jnp.mean(raw * raw, axis=1, keepdims=True) + EPSILON)
        attended[yi, :, lanes] = (raw * scale * hg_ref[:, lanes]).astype(BF16)
        if h % 2 == 1:
            pair = slice((h - 1) * HD, (h + 1) * HD)
            for d in range(1, NY):
                to = zi * NY + lax.rem(yi + d, NY)
                remote(
                    attended.at[yi, :, pair],
                    attended.at[yi, :, pair],
                    s_att,
                    r_att.at[yi],
                    seq=to,
                ).start()

    remote(
        weight.at[0 : (NZ - 1) * WCOLS], weight.at[0 : (NZ - 1) * WCOLS], s_w, r_w, seq=me
    ).wait_recv()

    @pl.loop(0, NY)
    def _(i):
        y = lax.rem(yi + NY - i, NY)

        @pl.when(i > 0)
        def _():
            remote(attended.at[y], attended.at[y], s_att, r_att.at[y], seq=me).wait_recv()

        partial[y] = nt(weight[...], attended[y]).astype(BF16)

        @pl.loop(1, NHEAD)
        def _(d):
            to = lax.rem(hd + d, NHEAD)
            remote(
                partial.at[y, pl.ds(pl.multiple_of(to * WCOLS, 32), WCOLS)],
                arrived.at[y, hd],
                s_part,
                r_part.at[y],
                head=to,
            ).start()

        arrived[y, hd] = partial[y, pl.ds(pl.multiple_of(hd * WCOLS, 32), WCOLS), :]

    @pl.loop(0, NY)
    def _(i):
        y = lax.rem(yi + NY - i, NY)
        remote(
            arrived.at[y, 0 : NHEAD - 1],
            arrived.at[y, 0 : NHEAD - 1],
            s_part,
            r_part.at[y],
            head=hd,
        ).wait_recv()
        total = arrived[y, 0].astype(F32)
        for h in range(1, NHEAD):
            total = total + arrived[y, h].astype(F32)
        column_out[y] = total.astype(BF16)

        @pl.when(i > 0)
        def _():
            remote(
                column_out.at[y], column_in.at[yi], s_col, r_col, seq=zi * NY + y
            ).start()

        @pl.when(i == 0)
        def _():
            column_in[yi] = total.astype(BF16)

    remote(
        column_in.at[0 : NY - 1], column_in.at[0 : NY - 1], s_col, r_col, seq=me
    ).wait_recv()
    for c in range(PART // HD):
        lanes = slice(c * HD, (c + 1) * HD)
        slab = column_in[...].astype(F32).reshape(PART, TOK)[c * HD : (c + 1) * HD, :]
        mid_ref[:, lanes] = (res_ref[:, lanes].astype(F32) + jnp.transpose(slab)).astype(BF16)

    remote(
        own_state.at[0:others], all_state.at[0:others], s_state, r_state, seq=me
    ).wait_send()
    remote(
        all_info.at[0:others], all_info.at[0:others], s_info, r_info, seq=me
    ).wait_send()
    remote(
        own_carry.at[0:others], all_carry.at[0:others], s_carry, r_carry, seq=me
    ).wait_send()
    remote(attended.at[0:3], attended.at[0:3], s_att, r_att.at[0], seq=me).wait_send()
    remote(
        weight.at[0 : (NZ - 1) * WCOLS], weight.at[0 : (NZ - 1) * WCOLS], s_w, r_w, seq=me
    ).wait_send()
    remote(
        arrived.at[:, 0 : NHEAD - 1],
        arrived.at[:, 0 : NHEAD - 1],
        s_part,
        r_part.at[0],
        head=hd,
    ).wait_send()
    remote(
        column_in.at[0 : NY - 1], column_in.at[0 : NY - 1], s_col, r_col, seq=me
    ).wait_send()


def attention(q, k, v, ld_t, doc, gain, w_t, residual):
    vmem = pl.BlockSpec(memory_space=pltpu.VMEM)
    dma = pltpu.SemaphoreType.DMA
    return pl.pallas_call(
        attention_kernel,
        out_shape=jax.ShapeDtypeStruct((TOK, PART), BF16),
        in_specs=[vmem] * 8,
        out_specs=vmem,
        scratch_shapes=[
            pltpu.VMEM((HEADS, TOK), F32),
            pltpu.VMEM((NSEQ, 32, HD), BF16),
            pltpu.VMEM((16, TOK), F32),
            pltpu.VMEM((NSEQ, 32, HD), BF16),
            pltpu.VMEM((NSEQ, 16, TOK), F32),
            pltpu.VMEM((NSEQ, 32, HD), BF16),
            pltpu.VMEM((NSEQ, 32, HD), BF16),
            pltpu.VMEM((TOK, HEADS * HD), F32),
            pltpu.VMEM((NY, TOK, HEADS * HD), BF16),
            pltpu.VMEM((NZ * WCOLS, HEADS * HD), BF16),
            pltpu.VMEM((NY, NZ * WCOLS, TOK), BF16),
            pltpu.VMEM((NY, NHEAD, WCOLS, TOK), BF16),
            pltpu.VMEM((NY, WCOLS, TOK), BF16),
            pltpu.VMEM((NY, WCOLS, TOK), BF16),
            dma,
            dma,
            dma,
            dma,
            dma,
            dma,
            dma,
            dma((NY,)),
            dma,
            dma,
            dma,
            dma((NY,)),
            dma,
            dma,
        ],
        compiler_params=pltpu.CompilerParams(
            collective_id=0, has_side_effects=True, vmem_limit_bytes=VMEM_LIMIT
        ),
        name="attention",
    )(q, k, v, ld_t, doc, gain, w_t, residual)


def expert_kernel(
    mid_ref,
    rout_ref,
    mix_ref,
    ng_ref,
    gate_hbm,
    up_hbm,
    down_hbm,
    out_ref,
    gate,
    up,
    down,
    outgoing,
    rows_in,
    normed,
    result,
    pair_in,
    pair_sum,
    plane_in,
    summed,
    returned,
    s_load,
    s_disp,
    r_disp,
    s_gath,
    r_gath,
    s_fwd,
    r_fwd,
    s_pair,
    r_pair,
    s_plane,
    r_plane,
    s_ret,
    r_ret,
):
    me, hd = lax.axis_index("seq"), lax.axis_index("head")
    xi, core = hd // 2, lax.rem(hd, 2)
    partner = xi * 2 + 1 - core
    group = me // GSRC
    barrier = greet(me, hd)
    loads = [
        pltpu.make_async_copy(gate_hbm, gate, s_load.at[0]),
        pltpu.make_async_copy(up_hbm, up, s_load.at[1]),
        pltpu.make_async_copy(down_hbm, down, s_load.at[2]),
    ]
    for load in loads:
        load.start()

    expert = lax.broadcasted_iota(jnp.int32, (NSEQ, TOK), 0)
    hits = [(expert == rout_ref[j : j + 1, :]).astype(F32) for j in range(2)]
    earlier = (
        lax.broadcasted_iota(jnp.int32, (TOK, TOK), 0)
        < lax.broadcasted_iota(jnp.int32, (TOK, TOK), 1)
    ).astype(BF16)
    count = nn((hits[0] + hits[1]).astype(BF16), earlier)
    places = [
        rout_ref[j : j + 1, :].astype(F32) * CAP
        + jnp.sum(hits[j] * count, axis=0, keepdims=True)
        for j in range(2)
    ]
    slot = lax.broadcasted_iota(jnp.int32, (NSEQ * CAP, TOK), 0).astype(F32)
    chosen = (slot == places[0]).astype(F32) + (slot == places[1]).astype(F32)
    outgoing[...] = (
        nn(chosen.astype(BF16), mid_ref[...]).astype(BF16).reshape(NSEQ, CAP, PART)
    )

    pl.semaphore_wait(barrier, NSEQ + NHEAD - 2)

    def my_rows(index):
        return pl.ds(pl.multiple_of(index * CAP, CAP), CAP)

    def group_rows(index):
        return pl.ds(pl.multiple_of(index * GROWS, GROWS), GROWS)

    @pl.loop(1, NSEQ)
    def _(d):
        to = lax.rem(me + d, NSEQ)
        remote(
            outgoing.at[to],
            rows_in.at[hd, my_rows(me)],
            s_disp,
            r_disp.at[group],
            seq=to,
        ).start()

    rows_in[hd, my_rows(me), :] = outgoing[me]

    def gather(i):
        g = lax.rem(group + NG - i, NG)
        part = group_rows(g)

        @pl.when(i == 0)
        def _():
            remote(
                outgoing.at[0 : GSRC - 1],
                outgoing.at[0 : GSRC - 1],
                s_disp,
                r_disp.at[g],
                seq=me,
            ).wait_recv()

        @pl.when(i > 0)
        def _():
            remote(
                outgoing.at[0:GSRC], outgoing.at[0:GSRC], s_disp, r_disp.at[g], seq=me
            ).wait_recv()

        for d in (2, 1, 3):
            to = lax.rem(xi + d, NX) * 2 + core
            remote(
                rows_in.at[hd, part],
                rows_in.at[hd, part],
                s_gath,
                r_gath.at[g, xi],
                head=to,
            ).start()
        remote(
            rows_in.at[hd, part], rows_in.at[hd, part], s_fwd, r_fwd.at[g], head=partner
        ).start()

    def forward(i):
        g = lax.rem(group + NG - i, NG)
        part = group_rows(g)
        for d in (1, 3, 2):
            x = lax.rem(xi + d, NX)
            block = rows_in.at[x * 2 + core, part]
            remote(block, block, s_gath, r_gath.at[g, x], head=hd).wait_recv()
            remote(block, block, s_fwd, r_fwd.at[g], head=partner).start()

    def serve(i):
        g = lax.rem(group + NG - i, NG)
        part = group_rows(g)

        @pl.when(i == 0)
        def _():
            for load in loads:
                load.wait()

        remote(
            rows_in.at[0:NX, 0:GROWS], rows_in.at[0:NX, 0:GROWS], s_fwd, r_fwd.at[g], head=hd
        ).wait_recv()
        squares = jnp.zeros((GROWS, HD), F32)
        for h in range(NHEAD):
            block = rows_in[h, part, :].astype(F32)
            block = block * block
            for c in range(PART // HD):
                squares = squares + block[:, c * HD : (c + 1) * HD]
        scale = lax.rsqrt(jnp.sum(squares, axis=1, keepdims=True) / D + EPSILON)
        for h in range(NHEAD):
            lanes = slice(h * PART, (h + 1) * PART)
            normed[:, lanes] = (
                rows_in[h, part, :].astype(F32) * scale * ng_ref[:, lanes]
            ).astype(BF16)
        gated = nt(normed[...], gate[...])
        upped = nt(normed[...], up[...])
        hidden = (gated / (1.0 + jnp.exp(-gated)) * upped).astype(BF16)
        for h in range(NHEAD):
            lanes = slice(h * PART, (h + 1) * PART)
            result[h % 2, h // 2, part, :] = nn(hidden, down[:, lanes]).astype(BF16)
        remote(
            result.at[1 - core, :, part],
            pair_in.at[:, part],
            s_pair,
            r_pair.at[g],
            head=partner,
        ).start()

    def reduce_pair(i):
        g = lax.rem(group + NG - i, NG)
        part = group_rows(g)
        remote(
            pair_in.at[:, part], pair_in.at[:, part], s_pair, r_pair.at[g], head=hd
        ).wait_recv()
        for d in (2, 1, 3, 0):
            x = lax.rem(xi + d, NX)
            pair_sum[x, part, :] = (
                result[core, x, part, :].astype(F32) + pair_in[x, part, :].astype(F32)
            ).astype(BF16)
            if d:
                remote(
                    pair_sum.at[x, part],
                    plane_in.at[xi, part],
                    s_plane,
                    r_plane.at[g],
                    head=x * 2 + core,
                ).start()

    def reduce_plane(i):
        g = lax.rem(group + NG - i, NG)
        part = group_rows(g)
        remote(
            plane_in.at[0 : NX - 1, part],
            plane_in.at[0 : NX - 1, part],
            s_plane,
            r_plane.at[g],
            head=hd,
        ).wait_recv()
        total = pair_sum[xi, part, :].astype(F32)
        for d in range(1, NX):
            total = total + plane_in[lax.rem(xi + d, NX), part, :].astype(F32)
        summed[part, :] = total.astype(BF16)

        @pl.loop(0, GSRC)
        def _(j):
            to = g * GSRC + j

            @pl.when(to != me)
            def _():
                remote(
                    summed.at[my_rows(to)], returned.at[my_rows(me)], s_ret, r_ret, seq=to
                ).start()

    def step(t, carry):
        pl.when(t < NG)(lambda: gather(t))
        pl.when((t >= 1) & (t < NG + 1))(lambda: forward(t - 1))
        pl.when((t >= 2) & (t < NG + 2))(lambda: serve(t - 2))
        pl.when((t >= 3) & (t < NG + 3))(lambda: reduce_pair(t - 3))
        pl.when(t >= 4)(lambda: reduce_plane(t - 4))
        return carry

    lax.fori_loop(0, NG + 4, step, 0)
    returned[my_rows(me), :] = summed[my_rows(me), :]

    lane = lax.broadcasted_iota(jnp.int32, (TOK, NSEQ * CAP), 1).astype(F32)
    picks = [(lane == columns(places[j])[:, 0:1]).astype(BF16) for j in range(2)]
    mixes = [columns(mix_ref[j : j + 1, :])[:, 0:1] for j in range(2)]
    others = (NSEQ - 1) * CAP
    remote(
        returned.at[0:others], returned.at[0:others], s_ret, r_ret, seq=me
    ).wait_recv()
    for c in range(PART // HD):
        lanes = slice(c * HD, (c + 1) * HD)
        out_ref[:, lanes] = (
            mid_ref[:, lanes].astype(F32)
            + (
                nn(picks[0], returned[:, lanes]) * mixes[0]
                + nn(picks[1], returned[:, lanes]) * mixes[1]
            )
        ).astype(BF16)

    remote(
        outgoing.at[0 : NSEQ - 1], outgoing.at[0 : NSEQ - 1], s_disp, r_disp.at[0], seq=me
    ).wait_send()
    remote(
        rows_in.at[0 : NX - 1], rows_in.at[0 : NX - 1], s_gath, r_gath.at[0, 0], head=hd
    ).wait_send()
    remote(rows_in.at[0:NX], rows_in.at[0:NX], s_fwd, r_fwd.at[0], head=hd).wait_send()
    remote(pair_in, pair_in, s_pair, r_pair.at[0], head=hd).wait_send()
    remote(
        plane_in.at[0 : NX - 1], plane_in.at[0 : NX - 1], s_plane, r_plane.at[0], head=hd
    ).wait_send()
    remote(
        returned.at[0:others], returned.at[0:others], s_ret, r_ret, seq=me
    ).wait_send()


def experts(middle, rout_t, mix_t, norm_gain, gate_t, up_t, down):
    vmem = pl.BlockSpec(memory_space=pltpu.VMEM)
    anywhere = pl.BlockSpec(memory_space=pl.ANY)
    dma = pltpu.SemaphoreType.DMA
    slots = NSEQ * CAP
    return pl.pallas_call(
        expert_kernel,
        out_shape=jax.ShapeDtypeStruct((TOK, PART), BF16),
        in_specs=[vmem] * 4 + [anywhere] * 3,
        out_specs=vmem,
        scratch_shapes=[
            pltpu.VMEM((FF, D), BF16),
            pltpu.VMEM((FF, D), BF16),
            pltpu.VMEM((FF, D), BF16),
            pltpu.VMEM((NSEQ, CAP, PART), BF16),
            pltpu.VMEM((NHEAD, slots, PART), BF16),
            pltpu.VMEM((GROWS, D), BF16),
            pltpu.VMEM((2, NX, slots, PART), BF16),
            pltpu.VMEM((NX, slots, PART), BF16),
            pltpu.VMEM((NX, slots, PART), BF16),
            pltpu.VMEM((NX, slots, PART), BF16),
            pltpu.VMEM((slots, PART), BF16),
            pltpu.VMEM((slots, PART), BF16),
            dma((3,)),
            dma,
            dma((NG,)),
            dma,
            dma((NG, NX)),
            dma,
            dma((NG,)),
            dma,
            dma((NG,)),
            dma,
            dma((NG,)),
            dma,
            dma,
        ],
        compiler_params=pltpu.CompilerParams(
            collective_id=1, has_side_effects=True, vmem_limit_bytes=VMEM_LIMIT
        ),
        name="experts",
    )(middle, rout_t, mix_t, norm_gain, gate_t, up_t, down)


def shards(
    queries,
    key_vectors,
    value_vectors,
    log_decay,
    doc_ids,
    head_gain,
    output_weight,
    residual,
    norm_gain,
    routing,
    route_weights,
    gate_weight,
    up_weight,
    down_weight,
):
    middle = attention(
        queries,
        key_vectors,
        value_vectors,
        log_decay.T,
        doc_ids.reshape(1, -1),
        head_gain.reshape(1, -1),
        output_weight.T,
        residual,
    )
    return experts(
        middle,
        routing.T,
        route_weights.T,
        norm_gain.reshape(1, -1),
        gate_weight[0].T,
        up_weight[0].T,
        down_weight[0],
    )


def solution(mesh):
    in_specs = (
        P("seq", "head"),
        P("seq", "head"),
        P("seq", "head"),
        P("seq", "head"),
        P("seq"),
        P("head"),
        P("head", "seq"),
        P("seq", "head"),
        P(),
        P("seq", None),
        P("seq", None),
        P("seq", None, "head"),
        P("seq", None, "head"),
        P("seq", "head", None),
    )
    return jax.shard_map(
        shards, mesh=mesh, in_specs=in_specs, out_specs=P("seq", "head"), check_vma=False
    )
```

time: 413 us -> 153 us (0.37)
  Pallas kernels: 0 us -> 150 us
  waiting for transfers between devices: 150 us -> 0 us
  blocking collectives: 89.9 us -> 0 us
  local copies, waits for them, and re-layouts: 49.6 us -> 1.54 us
  between operations: 45.7 us -> 0.02 us
  other arithmetic: 32.8 us -> 0 us
  matrix products: 27.5 us -> 0 us
  starting transfers between devices: 14.9 us -> 0 us
    pallas_call x0 -> x2, Pallas kernels: none -> 150 us  [the longest x1 86.1 us: attention(): pl.pallas_call(attention_kernel, out_shape=jax.ShapeDtypeStruct((TOK, PAR...]
    all_gather x4 -> x0, waiting for transfers between devices: 131 us -> none  [the longest x2 64.7 us: collected_together(): both, at, found = (lax.all_gather(jnp.concatenate(lines), axis), 0, {})]
    all_to_all x2 -> x0, blocking collectives: 64.3 us -> none  [the longest x1 41.9 us: sum_at_owner(): pieces = lax.all_to_all(in_blocks(array, dim, size), axis, 0, 0, tiled=True)]
    dot_general x6 -> x0, matrix products: 27.5 us -> none  [the longest x1 9.51 us: shards(): jnp.dot(hidden, down_local, preferred_element_type=jnp.float32)]
    all_to_all x2 -> x0, waiting for transfers between devices: 18.9 us -> none  [the longest x1 14.3 us: shards(): lax.all_to_all(summed_out.astype(jnp.bfloat16), SEQ, split_axis=0, concat...]
    all_to_all x2 -> x0, starting transfers between devices: 14.8 us -> none  [the longest x1 9.97 us: shards(): lax.all_to_all(summed_out.astype(jnp.bfloat16), SEQ, split_axis=0, concat...]
    all_gather x1 -> x0, blocking collectives: 14.3 us -> none  [gather_axes(): filled = lax.all_gather(filled, axes[number], axis=dim, tiled=True)]
    slice x11 -> x0, local copies, waits for them, and re-layouts: 13.2 us -> none  [the longest x6 7.96 us: entering(): running = combine(running, jax.tree.map(lambda part: part[k], pieces))]
  transfers between devices with their start and end apart: 6 -> 0, of which waited for: 6 -> 0; matrix products, arithmetic and copies ran while one was open for 9% -> 0% of each run, Pallas kernels for 0% -> 0%
where the time goes in v1:
time: 153 us; the launch traced here: 152 us
  Pallas kernels  150 us (98%)
  local copies, waits for them, and re-layouts  1.54 us (1%)
    pallas_call x1, Pallas kernels, attention(): pl.pallas_call(attention_kernel, out_shape=jax.ShapeDtypeStruct((TOK, PAR...  86.1 us
    pallas_call x1, Pallas kernels, experts(): pl.pallas_call(expert_kernel, out_shape=jax.ShapeDtypeStruct((TOK, PART),...  64.3 us

profile of v1, /device:TPU:2, one launch (start us, length us, event | category | flops | bytes accessed | tf_op | source)
XLA Modules:
  0.0 152.0 jit_solution(8228850240254247909)
XLA Ops:
  0.0 86.1 %attention.1.mid_ref = bf16[128,384]{1,0:T(8,128)(2,1)} custom-call(bf16[128,1024]{1,0:T(8,128)(2,1)} %q_ref.1, bf16[128,1024]{1,0:T(8,128)(2,1)} %k_ref.1, bf16[128,1024]{1,0:T(8,128)(2,1)} %v_ref.1, f32[8,128]{1,0:T(8,128)} %bitcast.19, s32[1,128]{1,0:T(1,128)} %bitcast.23, f32[1,1024]{1,0:T(1,128)} %bitcast.20, bf16[96,1024]{1,0:T(8,128)(2,1)} %bitcast.17, ...), custom_call_target="tpu_custom_call" | custom-call | tf_op jit(solution)/shard_map/attention/pallas_call | solution.py:301
  86.1 64.3 %experts.1 = bf16[128,384]{1,0:T(8,128)(2,1)} custom-call(bf16[128,384]{1,0:T(8,128)(2,1)} %attention.1.mid_ref, s32[2,128]{1,0:T(2,128)} %bitcast.21, f32[2,128]{1,0:T(2,128)} %bitcast.22, f32[1,3072]{1,0:T(1,128)} %bitcast.18, bf16[576,3072]{1,0:T(8,128)(2,1)} %bitcast.14, bf16[576,3072]{1,0:T(8,128)(2,1)} %bitcast.15, bf16[576,3072]{1,0:T(8,128)(2,1)} %bitcast.16), custom_call_target="tpu_custom_call" | custom-call | tf_op jit(solution)/shard_map/experts/pallas_call | solution.py:604
  150.4 1.5 %copy.16 = bf16[128,384]{1,0:T(8,128)(2,1)} copy(bf16[128,384]{1,0:T(8,128)(2,1)} %experts.1) | data formatting | bytes 196608

commit v2 on v1

--- a/solution.py
+++ b/solution.py
@@ -86,6 +86,8 @@
     attended,
     weight,
     partial,
+    paired,
+    summed,
     arrived,
     column_out,
     column_in,
@@ -99,6 +101,8 @@
     r_att,
     s_w,
     r_w,
+    s_pair,
+    r_pair,
     s_part,
     r_part,
     s_col,
@@ -106,6 +110,8 @@
 ):
     me, hd = lax.axis_index("seq"), lax.axis_index("head")
     zi, yi = me // NY, lax.rem(me, NY)
+    xi, core = hd // 2, lax.rem(hd, 2)
+    partner = xi * 2 + 1 - core
     barrier = greet(me, hd)
 
     rows = lax.broadcasted_iota(jnp.int32, (TOK, TOK), 0)
@@ -120,10 +126,10 @@
     doc_first, doc_last = doc[:, 0:1], doc[:, TOK - 1 : TOK]
     tail = jnp.exp(last - sums) * (doc == doc_last).astype(F32)
     gain = jnp.exp(last) * (doc_first == doc_last).astype(F32)
-    own_info[0:8, :] = jnp.broadcast_to(gain, (HEADS, TOK))
-    own_info[8:16, :] = jnp.where(
-        lax.broadcasted_iota(jnp.int32, (8, TOK), 0) == 0, doc_first, doc_last
-    )
+    lane = lax.broadcasted_iota(jnp.int32, (HEADS, TOK), 1)
+    info = jnp.where(lane < 32, gain, jnp.where(lane < 64, doc_first, doc_last))
+    for h in range(HEADS):
+        own_info[h] = info[h : h + 1, :]
     for h in range(HEADS):
         lanes = slice(h * HD, (h + 1) * HD)
         key_t = jnp.transpose(k_ref[:, lanes].astype(F32))
@@ -135,18 +141,33 @@
     @pl.loop(1, NSEQ)
     def _(d):
         to = lax.rem(me + d, NSEQ)
-        remote(own_info, all_info.at[me], s_info, r_info, seq=to).start()
+        remote(own_info.at[to // 4], all_info.at[me], s_info, r_info, seq=to).start()
         remote(own_state.at[to], all_state.at[me], s_state, r_state, seq=to).start()
 
     all_state[me] = own_state[me]
-    all_info[me] = own_info[...]
-
-    w_rows = pl.ds(pl.multiple_of(zi * WCOLS, 32), WCOLS)
-
-    @pl.loop(1, NZ)
-    def _(d):
-        to = lax.rem(zi + d, NZ) * NY + yi
-        remote(w_ref, weight.at[w_rows], s_w, r_w, seq=to).start()
+    all_info[me] = own_info[me // 4]
+
+    def w_rows(z, start=0, size=WCOLS):
+        return pl.ds(pl.multiple_of(lax.rem(z + NZ, NZ) * WCOLS + start, 16), size)
+
+    right = lax.rem(zi + 1, NZ) * NY + yi
+    left = lax.rem(zi + NZ - 1, NZ) * NY + yi
+    half = WCOLS // 2
+
+    def w_copy(rows, k, to, side):
+        block = weight.at[rows]
+        return remote(block, block, s_w, r_w.at[side, k], seq=to)
+
+    def w_step(k):
+        w_copy(w_rows(zi - 1 - k), k, me, 0).wait_recv()
+        from_left = w_rows(zi - 1 - k) if k < 2 else w_rows(zi - 1 - k, 0, half)
+        w_copy(from_left, k + 1, right, 0).start()
+        w_copy(w_rows(zi + 1 + k), k, me, 1).wait_recv()
+        from_right = w_rows(zi + 1 + k) if k < 2 else w_rows(zi + 1 + k, half, half)
+        w_copy(from_right, k + 1, left, 1).start()
+
+    remote(w_ref, weight.at[w_rows(zi)], s_w, r_w.at[0, 0], seq=right).start()
+    remote(w_ref, weight.at[w_rows(zi)], s_w, r_w.at[1, 0], seq=left).start()
 
     doc_rows = jnp.broadcast_to(doc, (TOK, TOK))
     kept = (cols <= rows) & (jnp.transpose(doc_rows) == doc_rows)
@@ -157,7 +178,7 @@
         factor = jnp.where(kept, jnp.exp(jnp.minimum(gap, 0.0)), 0.0)
         weighted = (nt(q_ref[:, lanes], k_ref[:, lanes]) * factor).astype(BF16)
         inner[:, lanes] = nn(weighted, v_ref[:, lanes])
-    weight[w_rows, :] = w_ref[...]
+    weight[w_rows(zi), :] = w_ref[...]
 
     others = NSEQ - 1
     remote(
@@ -166,18 +187,20 @@
     remote(
         all_info.at[0:others], all_info.at[0:others], s_info, r_info, seq=me
     ).wait_recv()
-    my_head = me // 4
 
     def scan(b, carry):
         carried, before = carry
         own_carry[b] = carried.astype(BF16)
-        gain_row = all_info[b, pl.ds(my_head, 1), :]
-        docs = all_info[b, 8:16, :]
-        through = jnp.where(docs[0:1, :] == before, gain_row, 0.0)
-        return all_state[b].astype(F32) + through * carried, docs[1:2, :]
+        row = all_info[b]
+        through = jnp.where(row[:, 32:33] == before, row[:, 0:1], 0.0)
+        return all_state[b].astype(F32) + through * carried, row[:, 64:65]
 
     lax.fori_loop(
-        0, NSEQ, scan, (jnp.zeros((32, HD), F32), jnp.full((1, HD), -1.0, F32))
+        0,
+        NSEQ,
+        scan,
+        (jnp.zeros((32, HD), F32), jnp.full((1, 1), -1.0, F32)),
+        unroll=4,
     )
 
     @pl.loop(1, NSEQ)
@@ -186,12 +209,14 @@
         remote(own_carry.at[to], all_carry.at[me], s_carry, r_carry, seq=to).start()
 
     all_carry[me] = own_carry[me]
-    before_doc = all_info[jnp.maximum(me - 1, 0), 8:16, :][1:2, :]
-    before_doc = jnp.where(jnp.full((1, TOK), me, jnp.int32) == 0, -1.0, before_doc)
+    before_doc = all_info[jnp.maximum(me - 1, 0)][:, 64:65]
+    before_doc = jnp.where(jnp.full((1, 1), me, jnp.int32) == 0, -1.0, before_doc)
+    w_step(0)
     reach = jnp.exp(decay[...]) * (doc == before_doc).astype(F32)
     remote(
         own_carry.at[0:others], all_carry.at[0:others], s_carry, r_carry, seq=me
     ).wait_recv()
+    w_step(1)
     for h in range(HEADS):
         lanes = slice(h * HD, (h + 1) * HD)
         carried = all_carry[4 * h : 4 * h + 4].reshape(HD, HD)
@@ -210,46 +235,54 @@
                     seq=to,
                 ).start()
 
-    remote(
-        weight.at[0 : (NZ - 1) * WCOLS], weight.at[0 : (NZ - 1) * WCOLS], s_w, r_w, seq=me
-    ).wait_recv()
-
-    @pl.loop(0, NY)
-    def _(i):
+    w_step(2)
+    w_copy(w_rows(zi + 4, 0, half), 3, me, 0).wait_recv()
+    w_copy(w_rows(zi + 4, half, half), 3, me, 1).wait_recv()
+
+    def project(i):
         y = lax.rem(yi + NY - i, NY)
 
         @pl.when(i > 0)
         def _():
             remote(attended.at[y], attended.at[y], s_att, r_att.at[y], seq=me).wait_recv()
 
-        partial[y] = nt(weight[...], attended[y]).astype(BF16)
-
-        @pl.loop(1, NHEAD)
-        def _(d):
-            to = lax.rem(hd + d, NHEAD)
-            remote(
-                partial.at[y, pl.ds(pl.multiple_of(to * WCOLS, 32), WCOLS)],
-                arrived.at[y, hd],
-                s_part,
-                r_part.at[y],
-                head=to,
-            ).start()
-
-        arrived[y, hd] = partial[y, pl.ds(pl.multiple_of(hd * WCOLS, 32), WCOLS), :]
-
-    @pl.loop(0, NY)
-    def _(i):
+        partial[y] = nt(weight[...], attended[y]).astype(BF16).reshape(NX, 2, WCOLS, TOK)
+        remote(
+            partial.at[y, :, 1 - core], paired.at[y], s_pair, r_pair.at[y], head=partner
+        ).start()
+
+    def pair_sum(i):
+        y = lax.rem(yi + NY - i, NY)
+        remote(paired.at[y], paired.at[y], s_pair, r_pair.at[y], head=hd).wait_recv()
+        for d in (2, 1, 3, 0):
+            x = lax.rem(xi + d, NX)
+            both = (
+                partial[y, x, core].astype(F32) + paired[y, x].astype(F32)
+            ).astype(BF16)
+            if d:
+                summed[y, x] = both
+                remote(
+                    summed.at[y, x],
+                    arrived.at[y, xi],
+                    s_part,
+                    r_part.at[y],
+                    head=x * 2 + core,
+                ).start()
+            else:
+                arrived[y, xi] = both
+
+    def plane_sum(i):
         y = lax.rem(yi + NY - i, NY)
         remote(
-            arrived.at[y, 0 : NHEAD - 1],
-            arrived.at[y, 0 : NHEAD - 1],
+            arrived.at[y, 0 : NX - 1],
+            arrived.at[y, 0 : NX - 1],
             s_part,
             r_part.at[y],
             head=hd,
         ).wait_recv()
         total = arrived[y, 0].astype(F32)
-        for h in range(1, NHEAD):
-            total = total + arrived[y, h].astype(F32)
+        for x in range(1, NX):
+            total = total + arrived[y, x].astype(F32)
         column_out[y] = total.astype(BF16)
 
         @pl.when(i > 0)
@@ -262,6 +295,13 @@
         def _():
             column_in[yi] = total.astype(BF16)
 
+    def step(t, carry):
+        pl.when(t < NY)(lambda: project(t))
+        pl.when((t >= 1) & (t < NY + 1))(lambda: pair_sum(t - 1))
+        pl.when(t >= 2)(lambda: plane_sum(t - 2))
+        return carry
+
+    lax.fori_loop(0, NY + 2, step, 0)
     remote(
         column_in.at[0 : NY - 1], column_in.at[0 : NY - 1], s_col, r_col, seq=me
     ).wait_recv()
@@ -280,12 +320,11 @@
         own_carry.at[0:others], all_carry.at[0:others], s_carry, r_carry, seq=me
     ).wait_send()
     remote(attended.at[0:3], attended.at[0:3], s_att, r_att.at[0], seq=me).wait_send()
-    remote(
-        weight.at[0 : (NZ - 1) * WCOLS], weight.at[0 : (NZ - 1) * WCOLS], s_w, r_w, seq=me
-    ).wait_send()
-    remote(
-        arrived.at[:, 0 : NHEAD - 1],
-        arrived.at[:, 0 : NHEAD - 1],
+    w_copy(pl.ds(0, (NZ - 1) * WCOLS), 0, me, 0).wait_send()
+    remote(paired, paired, s_pair, r_pair.at[0], head=hd).wait_send()
+    remote(
+        arrived.at[:, 0 : NX - 1],
+        arrived.at[:, 0 : NX - 1],
         s_part,
         r_part.at[0],
         head=hd,
@@ -306,16 +345,18 @@
         scratch_shapes=[
             pltpu.VMEM((HEADS, TOK), F32),
             pltpu.VMEM((NSEQ, 32, HD), BF16),
-            pltpu.VMEM((16, TOK), F32),
+            pltpu.VMEM((HEADS, 1, TOK), F32),
             pltpu.VMEM((NSEQ, 32, HD), BF16),
-            pltpu.VMEM((NSEQ, 16, TOK), F32),
+            pltpu.VMEM((NSEQ, 1, TOK), F32),
             pltpu.VMEM((NSEQ, 32, HD), BF16),
             pltpu.VMEM((NSEQ, 32, HD), BF16),
             pltpu.VMEM((TOK, HEADS * HD), F32),
             pltpu.VMEM((NY, TOK, HEADS * HD), BF16),
             pltpu.VMEM((NZ * WCOLS, HEADS * HD), BF16),
-            pltpu.VMEM((NY, NZ * WCOLS, TOK), BF16),
-            pltpu.VMEM((NY, NHEAD, WCOLS, TOK), BF16),
+            pltpu.VMEM((NY, NX, 2, WCOLS, TOK), BF16),
+            pltpu.VMEM((NY, NX, WCOLS, TOK), BF16),
+            pltpu.VMEM((NY, NX, WCOLS, TOK), BF16),
+            pltpu.VMEM((NY, NX, WCOLS, TOK), BF16),
             pltpu.VMEM((NY, WCOLS, TOK), BF16),
             pltpu.VMEM((NY, WCOLS, TOK), BF16),
             dma,
@@ -327,7 +368,9 @@
             dma,
             dma((NY,)),
             dma,
-            dma,
+            dma((2, 4)),
+            dma,
+            dma((NY,)),
             dma,
             dma((NY,)),
             dma,

time: 153 us -> 123 us (0.80)
  Pallas kernels: 150 us -> 120 us
    pallas_call x1, Pallas kernels: 86.1 us -> 58.8 us  [attention(): pl.pallas_call(attention_kernel, out_shape=jax.ShapeDtypeStruct((TOK, PAR...]
    pallas_call x1, Pallas kernels: 64.3 us -> 61.4 us  [experts(): pl.pallas_call(expert_kernel, out_shape=jax.ShapeDtypeStruct((TOK, PART),...]
where the time goes in v2:
time: 123 us; the launch traced here: 122 us
  Pallas kernels  120 us (98%)
  local copies, waits for them, and re-layouts  1.54 us (1%)
    pallas_call x1, Pallas kernels, experts(): pl.pallas_call(expert_kernel, out_shape=jax.ShapeDtypeStruct((TOK, PART),...  61.4 us
    pallas_call x1, Pallas kernels, attention(): pl.pallas_call(attention_kernel, out_shape=jax.ShapeDtypeStruct((TOK, PAR...  58.8 us

profile of v2, /device:TPU:2, one launch (start us, length us, event | category | flops | bytes accessed | tf_op | source)
XLA Modules:
  0.0 121.7 jit_solution(13098772360807849932)
XLA Ops:
  0.0 58.8 %attention.1.mid_ref = bf16[128,384]{1,0:T(8,128)(2,1)} custom-call(bf16[128,1024]{1,0:T(8,128)(2,1)} %q_ref.1, bf16[128,1024]{1,0:T(8,128)(2,1)} %k_ref.1, bf16[128,1024]{1,0:T(8,128)(2,1)} %v_ref.1, f32[8,128]{1,0:T(8,128)} %bitcast.19, s32[1,128]{1,0:T(1,128)} %bitcast.23, f32[1,1024]{1,0:T(1,128)} %bitcast.20, bf16[96,1024]{1,0:T(8,128)(2,1)} %bitcast.17, ...), custom_call_target="tpu_custom_call" | custom-call | tf_op jit(solution)/shard_map/attention/pallas_call | solution.py:340
  58.8 61.4 %experts.1 = bf16[128,384]{1,0:T(8,128)(2,1)} custom-call(bf16[128,384]{1,0:T(8,128)(2,1)} %attention.1.mid_ref, s32[2,128]{1,0:T(2,128)} %bitcast.21, f32[2,128]{1,0:T(2,128)} %bitcast.22, f32[1,3072]{1,0:T(1,128)} %bitcast.18, bf16[576,3072]{1,0:T(8,128)(2,1)} %bitcast.14, bf16[576,3072]{1,0:T(8,128)(2,1)} %bitcast.15, bf16[576,3072]{1,0:T(8,128)(2,1)} %bitcast.16), custom_call_target="tpu_custom_call" | custom-call | tf_op jit(solution)/shard_map/experts/pallas_call | solution.py:647
  120.1 1.5 %copy.16 = bf16[128,384]{1,0:T(8,128)(2,1)} copy(bf16[128,384]{1,0:T(8,128)(2,1)} %experts.1) | data formatting | bytes 196608

commit v3 on v2

v3 whole, which is shorter than its diff:
```python
import functools

import jax
import jax.numpy as jnp
from jax import lax
from jax.experimental import pallas as pl
from jax.experimental.pallas import tpu as pltpu
from jax.sharding import PartitionSpec as P

MESH = pl.DeviceIdType.MESH
F32, BF16 = jnp.float32, jnp.bfloat16
EPSILON = 1e-06
NZ, NY, NX = 8, 4, 4
NSEQ, NHEAD = NZ * NY, 2 * NX
TOK, HEADS, HD = 128, 8, 128
WCOLS = 96
PART = 384
D = PART * NHEAD
CAP = 16
NG = 4
GSRC = NSEQ // NG
GROWS = GSRC * CAP
SLOTS = NSEQ * CAP
FF = 576
VMEM_LIMIT = 60 * 1024 * 1024


def nt(a, b):
    return lax.dot_general(a, b, (((1,), (1,)), ((), ())), preferred_element_type=F32)


def nn(a, b):
    return jnp.dot(a, b, preferred_element_type=F32)


def remote(src, dst, send_sem, recv_sem, **device):
    return pltpu.make_async_remote_copy(
        src_ref=src,
        dst_ref=dst,
        send_sem=send_sem,
        recv_sem=recv_sem,
        device_id=device,
        device_id_type=MESH,
    )


def greet(me, hd):
    barrier = pltpu.get_barrier_semaphore()

    @pl.loop(1, NSEQ)
    def _(d):
        pl.semaphore_signal(
            barrier, inc=1, device_id={"seq": lax.rem(me + d, NSEQ)}, device_id_type=MESH
        )

    @pl.loop(1, NHEAD)
    def _(d):
        pl.semaphore_signal(
            barrier, inc=1, device_id={"head": lax.rem(hd + d, NHEAD)}, device_id_type=MESH
        )

    return barrier


def turn(i):
    return i + i // 2 - 2 * (i // 3)


def columns(row):
    return jnp.transpose(jnp.broadcast_to(row, (TOK, TOK)))


def layer_kernel(
    q_ref,
    k_ref,
    v_ref,
    ld_ref,
    doc_ref,
    hg_ref,
    w_ref,
    res_ref,
    rout_ref,
    mix_ref,
    ng_ref,
    gate_hbm,
    up_hbm,
    down_hbm,
    out_ref,
    decay,
    own_state,
    own_info,
    all_state,
    all_info,
    own_carry,
    all_carry,
    inner,
    attended,
    weight,
    partial,
    paired,
    half_sum,
    arrived,
    column_out,
    column_in,
    middle,
    chosen_rows,
    picks,
    mixes,
    gate,
    up,
    down,
    outgoing,
    rows_in,
    normed,
    result,
    pair_in,
    far_sum,
    ring_in,
    near_sum,
    plane_in,
    summed,
    returned,
    s_state,
    r_state,
    s_info,
    r_info,
    s_carry,
    r_carry,
    s_att,
    r_att,
    s_w,
    r_w,
    s_pp,
    r_pp,
    s_part,
    r_part,
    s_col,
    r_col,
    s_load,
    s_disp,
    r_disp,
    s_gath,
    r_gath,
    s_fwd,
    r_fwd,
    s_pair,
    r_pair,
    s_ring,
    r_ring,
    s_plane,
    r_plane,
    s_ret,
    r_ret,
):
    me, hd = lax.axis_index("seq"), lax.axis_index("head")
    zi, yi = me // NY, lax.rem(me, NY)
    xi, core = hd // 2, lax.rem(hd, 2)
    partner = xi * 2 + 1 - core
    group = me // GSRC
    barrier = greet(me, hd)
    loads = [
        pltpu.make_async_copy(gate_hbm, gate, s_load.at[0]),
        pltpu.make_async_copy(up_hbm, up, s_load.at[1]),
        pltpu.make_async_copy(down_hbm, down, s_load.at[2]),
    ]
    for load in loads:
        load.start()

    rows = lax.broadcasted_iota(jnp.int32, (TOK, TOK), 0)
    cols = lax.broadcasted_iota(jnp.int32, (TOK, TOK), 1)
    upper = (rows <= cols).astype(F32)
    sums = jnp.dot(
        ld_ref[...], upper, preferred_element_type=F32, precision=lax.Precision.HIGHEST
    )
    decay[...] = sums
    last = sums[:, TOK - 1 : TOK]
    doc = doc_ref[...].astype(F32)
    doc_first, doc_last = doc[:, 0:1], doc[:, TOK - 1 : TOK]
    tail = jnp.exp(last - sums) * (doc == doc_last).astype(F32)
    gain = jnp.exp(last) * (doc_first == doc_last).astype(F32)
    lane = lax.broadcasted_iota(jnp.int32, (HEADS, TOK), 1)
    info = jnp.where(lane < 32, gain, jnp.where(lane < 64, doc_first, doc_last))
    for h in range(HEADS):
        own_info[h] = info[h : h + 1, :]
    for h in range(HEADS):
        lanes = slice(h * HD, (h + 1) * HD)
        key_t = jnp.transpose(k_ref[:, lanes].astype(F32))
        state = nn((key_t * tail[h : h + 1, :]).astype(BF16), v_ref[:, lanes])
        own_state[4 * h : 4 * h + 4] = state.astype(BF16).reshape(4, 32, HD)

    pl.semaphore_wait(barrier, NSEQ + NHEAD - 2)

    @pl.loop(1, NSEQ)
    def _(d):
        to = lax.rem(me + d, NSEQ)
        remote(own_info.at[to // 4], all_info.at[me], s_info, r_info, seq=to).start()
        remote(own_state.at[to], all_state.at[me], s_state, r_state, seq=to).start()

    all_state[me] = own_state[me]
    all_info[me] = own_info[me // 4]

    def w_rows(z, start=0, size=WCOLS):
        return pl.ds(pl.multiple_of(lax.rem(z + NZ, NZ) * WCOLS + start, 16), size)

    right = lax.rem(zi + 1, NZ) * NY + yi
    left = lax.rem(zi + NZ - 1, NZ) * NY + yi
    half = WCOLS // 2

    def w_copy(rows, k, to, side):
        block = weight.at[rows]
        return remote(block, block, s_w, r_w.at[side, k], seq=to)

    def w_step(k):
        w_copy(w_rows(zi - 1 - k), k, me, 0).wait_recv()
        from_left = w_rows(zi - 1 - k) if k < 2 else w_rows(zi - 1 - k, 0, half)
        w_copy(from_left, k + 1, right, 0).start()
        w_copy(w_rows(zi + 1 + k), k, me, 1).wait_recv()
        from_right = w_rows(zi + 1 + k) if k < 2 else w_rows(zi + 1 + k, half, half)
        w_copy(from_right, k + 1, left, 1).start()

    remote(w_ref, weight.at[w_rows(zi)], s_w, r_w.at[0, 0], seq=right).start()
    remote(w_ref, weight.at[w_rows(zi)], s_w, r_w.at[1, 0], seq=left).start()

    doc_rows = jnp.broadcast_to(doc, (TOK, TOK))
    kept = (cols <= rows) & (jnp.transpose(doc_rows) == doc_rows)
    for h in range(HEADS):
        lanes = slice(h * HD, (h + 1) * HD)
        decay_row = jnp.broadcast_to(decay[h : h + 1, :], (TOK, TOK))
        gap = jnp.transpose(decay_row) - decay_row
        factor = jnp.where(kept, jnp.exp(jnp.minimum(gap, 0.0)), 0.0)
        weighted = (nt(q_ref[:, lanes], k_ref[:, lanes]) * factor).astype(BF16)
        inner[:, lanes] = nn(weighted, v_ref[:, lanes])
    weight[w_rows(zi), :] = w_ref[...]
    expert = lax.broadcasted_iota(jnp.int32, (NSEQ, TOK), 0)
    hits = [(expert == rout_ref[j : j + 1, :]).astype(F32) for j in range(2)]
    earlier = (
        lax.broadcasted_iota(jnp.int32, (TOK, TOK), 0)
        < lax.broadcasted_iota(jnp.int32, (TOK, TOK), 1)
    ).astype(BF16)
    count = nn((hits[0] + hits[1]).astype(BF16), earlier)
    places = [
        rout_ref[j : j + 1, :].astype(F32) * CAP
        + jnp.sum(hits[j] * count, axis=0, keepdims=True)
        for j in range(2)
    ]
    slot = lax.broadcasted_iota(jnp.int32, (NSEQ * CAP, TOK), 0).astype(F32)
    chosen = (slot == places[0]).astype(F32) + (slot == places[1]).astype(F32)
    chosen_rows[...] = chosen.astype(BF16)
    lane = lax.broadcasted_iota(jnp.int32, (TOK, NSEQ * CAP), 1).astype(F32)
    for j in range(2):
        picks[j] = (lane == columns(places[j])[:, 0:1]).astype(BF16)
        mixes[j] = columns(mix_ref[j : j + 1, :])


    others = NSEQ - 1
    remote(
        own_state.at[0:others], all_state.at[0:others], s_state, r_state, seq=me
    ).wait_recv()
    remote(
        all_info.at[0:others], all_info.at[0:others], s_info, r_info, seq=me
    ).wait_recv()

    def scan(b, carry):
        carried, before = carry
        own_carry[b] = carried.astype(BF16)
        row = all_info[b]
        through = jnp.where(row[:, 32:33] == before, row[:, 0:1], 0.0)
        return all_state[b].astype(F32) + through * carried, row[:, 64:65]

    lax.fori_loop(
        0,
        NSEQ,
        scan,
        (jnp.zeros((32, HD), F32), jnp.full((1, 1), -1.0, F32)),
        unroll=4,
    )

    @pl.loop(1, NSEQ)
    def _(d):
        to = lax.rem(me + d, NSEQ)
        remote(own_carry.at[to], all_carry.at[me], s_carry, r_carry, seq=to).start()

    all_carry[me] = own_carry[me]
    before_doc = all_info[jnp.maximum(me - 1, 0)][:, 64:65]
    before_doc = jnp.where(jnp.full((1, 1), me, jnp.int32) == 0, -1.0, before_doc)
    w_step(0)
    reach = jnp.exp(decay[...]) * (doc == before_doc).astype(F32)
    remote(
        own_carry.at[0:others], all_carry.at[0:others], s_carry, r_carry, seq=me
    ).wait_recv()
    w_step(1)
    y_up = zi * NY + lax.rem(yi + 1, NY)
    y_down = zi * NY + lax.rem(yi + NY - 1, NY)

    def att_half(y, part):
        return attended.at[lax.rem(y + NY, NY), :, part * 512 : (part + 1) * 512]

    def att_wait(block, side, part):
        remote(block, block, s_att, r_att.at[side, part], seq=me).wait_recv()

    for h in range(HEADS):
        lanes = slice(h * HD, (h + 1) * HD)
        carried = all_carry[4 * h : 4 * h + 4].reshape(HD, HD)
        raw = inner[:, lanes] + nn(q_ref[:, lanes], carried) * columns(reach[h : h + 1, :])
        scale = lax.rsqrt(jnp.mean(raw * raw, axis=1, keepdims=True) + EPSILON)
        attended[yi, :, lanes] = (raw * scale * hg_ref[:, lanes]).astype(BF16)
        if h % 2 == 1:
            pair = slice((h - 1) * HD, (h + 1) * HD)
            block = attended.at[yi, :, pair]
            remote(block, block, s_att, r_att.at[0, h // 4], seq=y_up).start()
            remote(block, block, s_att, r_att.at[1, h // 4], seq=y_down).start()

    block = att_half(yi - 1, 0)
    att_wait(block, 0, 0)
    remote(block, block, s_att, r_att.at[2, 0], seq=y_up).start()
    w_step(2)
    block = att_half(yi + 1, 1)
    att_wait(block, 1, 1)
    remote(block, block, s_att, r_att.at[2, 1], seq=y_down).start()
    w_copy(w_rows(zi + 4, 0, half), 3, me, 0).wait_recv()
    w_copy(w_rows(zi + 4, half, half), 3, me, 1).wait_recv()

    def project(i):
        y = lax.rem(yi + NY - turn(i), NY)
        pl.when(i == 1)(lambda: att_wait(att_half(yi - 1, 1), 0, 1))
        pl.when(i == 2)(lambda: att_wait(att_half(yi + 1, 0), 1, 0))

        @pl.when(i == 3)
        def _():
            att_wait(att_half(yi + 2, 0), 2, 0)
            att_wait(att_half(yi + 2, 1), 2, 1)

        partial[y] = nt(weight[...], attended[y]).astype(BF16).reshape(NX, 2, WCOLS, TOK)
        remote(
            partial.at[y, :, 1 - core], paired.at[y], s_pp, r_pp.at[y], head=partner
        ).start()

    def pair_sum(i):
        y = lax.rem(yi + NY - turn(i), NY)
        remote(paired.at[y], paired.at[y], s_pp, r_pp.at[y], head=hd).wait_recv()
        for d in (2, 1, 3, 0):
            x = lax.rem(xi + d, NX)
            both = (
                partial[y, x, core].astype(F32) + paired[y, x].astype(F32)
            ).astype(BF16)
            if d:
                half_sum[y, x] = both
                remote(
                    half_sum.at[y, x],
                    arrived.at[y, xi],
                    s_part,
                    r_part.at[y],
                    head=x * 2 + core,
                ).start()
            else:
                arrived[y, xi] = both

    def plane_sum(i):
        y = lax.rem(yi + NY - turn(i), NY)
        remote(
            arrived.at[y, 0 : NX - 1],
            arrived.at[y, 0 : NX - 1],
            s_part,
            r_part.at[y],
            head=hd,
        ).wait_recv()
        total = arrived[y, 0].astype(F32)
        for x in range(1, NX):
            total = total + arrived[y, x].astype(F32)
        column_out[y] = total.astype(BF16)

        @pl.when(i > 0)
        def _():
            remote(
                column_out.at[y], column_in.at[yi], s_col, r_col, seq=zi * NY + y
            ).start()

        @pl.when(i == 0)
        def _():
            column_in[yi] = total.astype(BF16)

    def project_step(t, carry):
        pl.when(t < NY)(lambda: project(t))
        pl.when((t >= 1) & (t < NY + 1))(lambda: pair_sum(t - 1))
        pl.when(t >= 2)(lambda: plane_sum(t - 2))
        return carry

    lax.fori_loop(0, NY + 2, project_step, 0)
    remote(
        column_in.at[0 : NY - 1], column_in.at[0 : NY - 1], s_col, r_col, seq=me
    ).wait_recv()
    for c in range(PART // HD):
        lanes = slice(c * HD, (c + 1) * HD)
        slab = column_in[...].astype(F32).reshape(PART, TOK)[c * HD : (c + 1) * HD, :]
        middle[:, lanes] = (res_ref[:, lanes].astype(F32) + jnp.transpose(slab)).astype(BF16)

    outgoing[...] = (
        nn(chosen_rows[...], middle[...]).astype(BF16).reshape(NSEQ, CAP, PART)
    )

    def my_rows(index):
        return pl.ds(pl.multiple_of(index * CAP, CAP), CAP)

    x_up = lax.rem(xi + 1, NX) * 2 + core
    x_down = lax.rem(xi + NX - 1, NX) * 2 + core
    x_far = lax.rem(xi + 2, NX) * 2 + core

    def half_rows(index, side):
        start = index * GROWS + side * (GROWS // 2)
        return pl.ds(pl.multiple_of(start, GROWS // 2), GROWS // 2)

    def group_rows(index):
        return pl.ds(pl.multiple_of(index * GROWS, GROWS), GROWS)

    @pl.loop(1, NSEQ)
    def _(n):
        to = lax.rem(group + turn(n // GSRC), NG) * GSRC + lax.rem(me + n, GSRC)
        remote(
            outgoing.at[to],
            rows_in.at[hd, my_rows(me)],
            s_disp,
            r_disp.at[group],
            seq=to,
        ).start()

    rows_in[hd, my_rows(me), :] = outgoing[me]

    def gather(i):
        g = lax.rem(group + NG - turn(i), NG)
        part = group_rows(g)

        @pl.when(i == 0)
        def _():
            remote(
                outgoing.at[0 : GSRC - 1],
                outgoing.at[0 : GSRC - 1],
                s_disp,
                r_disp.at[g],
                seq=me,
            ).wait_recv()

        @pl.when(i > 0)
        def _():
            remote(
                outgoing.at[0:GSRC], outgoing.at[0:GSRC], s_disp, r_disp.at[g], seq=me
            ).wait_recv()

        block = rows_in.at[hd, part]
        remote(block, block, s_gath, r_gath.at[g, 0], head=x_up).start()
        remote(block, block, s_gath, r_gath.at[g, 1], head=x_down).start()
        remote(block, block, s_fwd, r_fwd.at[g], head=partner).start()

    def forward(i):
        g = lax.rem(group + NG - turn(i), NG)
        part = group_rows(g)
        for side, source, to in ((0, x_down, x_up), (1, x_up, x_down)):
            block = rows_in.at[source, part]
            remote(block, block, s_gath, r_gath.at[g, side], head=hd).wait_recv()
            piece = rows_in.at[source, half_rows(g, side)]
            remote(piece, piece, s_gath, r_gath.at[g, 2 + side], head=to).start()
            remote(block, block, s_fwd, r_fwd.at[g], head=partner).start()

    def forward_far(i):
        g = lax.rem(group + NG - turn(i), NG)
        for side in range(2):
            piece = rows_in.at[x_far, half_rows(g, side)]
            remote(piece, piece, s_gath, r_gath.at[g, 2 + side], head=hd).wait_recv()
        block = rows_in.at[x_far, group_rows(g)]
        remote(block, block, s_fwd, r_fwd.at[g], head=partner).start()

    def serve(i):
        g = lax.rem(group + NG - turn(i), NG)
        part = group_rows(g)

        @pl.when(i == 0)
        def _():
            for load in loads:
                load.wait()

        remote(
            rows_in.at[0:NX, 0:GROWS], rows_in.at[0:NX, 0:GROWS], s_fwd, r_fwd.at[g], head=hd
        ).wait_recv()
        squares = jnp.zeros((GROWS, HD), F32)
        for h in range(NHEAD):
            block = rows_in[h, part, :].astype(F32)
            block = block * block
            for c in range(PART // HD):
                squares = squares + block[:, c * HD : (c + 1) * HD]
        scale = lax.rsqrt(jnp.sum(squares, axis=1, keepdims=True) / D + EPSILON)
        for h in range(NHEAD):
            lanes = slice(h * PART, (h + 1) * PART)
            normed[:, lanes] = (
                rows_in[h, part, :].astype(F32) * scale * ng_ref[:, lanes]
            ).astype(BF16)
        gated = nt(normed[...], gate[...])
        upped = nt(normed[...], up[...])
        hidden = (gated / (1.0 + jnp.exp(-gated)) * upped).astype(BF16)
        for h in range(NHEAD):
            lanes = slice(h * PART, (h + 1) * PART)
            result[h % 2, h // 2, part, :] = nn(hidden, down[:, lanes]).astype(BF16)
        remote(
            result.at[1 - core, :, part],
            pair_in.at[:, part],
            s_pair,
            r_pair.at[g],
            head=partner,
        ).start()

    def both_cores(x, rows):
        return result[core, x, rows, :].astype(F32) + pair_in[x, rows, :].astype(F32)

    def reduce_pair(i):
        g = lax.rem(group + NG - turn(i), NG)
        part = group_rows(g)
        remote(
            pair_in.at[:, part], pair_in.at[:, part], s_pair, r_pair.at[g], head=hd
        ).wait_recv()
        far_sum[part, :] = both_cores(x_far // 2, part).astype(BF16)
        for side, to in ((0, x_up), (1, x_down)):
            piece = half_rows(g, side)
            remote(
                far_sum.at[piece],
                ring_in.at[piece],
                s_ring,
                r_ring.at[g, side],
                head=to,
            ).start()

    def reduce_mid(i):
        g = lax.rem(group + NG - turn(i), NG)
        part = group_rows(g)
        for side, to in ((0, x_up), (1, x_down)):
            piece, other = half_rows(g, side), half_rows(g, 1 - side)
            near_sum[side, other, :] = both_cores(to // 2, other).astype(BF16)
            remote(
                ring_in.at[piece], ring_in.at[piece], s_ring, r_ring.at[g, side], head=hd
            ).wait_recv()
            near_sum[side, piece, :] = (
                both_cores(to // 2, piece) + ring_in[piece, :].astype(F32)
            ).astype(BF16)
            remote(
                near_sum.at[side, part],
                plane_in.at[side, part],
                s_plane,
                r_plane.at[g],
                head=to,
            ).start()

    def reduce_plane(i):
        g = lax.rem(group + NG - turn(i), NG)
        part = group_rows(g)
        remote(
            plane_in.at[:, part], plane_in.at[:, part], s_plane, r_plane.at[g], head=hd
        ).wait_recv()
        total = both_cores(xi, part)
        for side in range(2):
            total = total + plane_in[side, part, :].astype(F32)
        summed[part, :] = total.astype(BF16)

        @pl.loop(0, GSRC)
        def _(j):
            to = g * GSRC + j

            @pl.when(to != me)
            def _():
                remote(
                    summed.at[my_rows(to)], returned.at[my_rows(me)], s_ret, r_ret, seq=to
                ).start()

    stages = (
        gather,
        forward,
        forward_far,
        serve,
        reduce_pair,
        reduce_mid,
        reduce_plane,
    )

    def step(t, carry):
        for number, stage in enumerate(stages):
            pl.when((t >= number) & (t < number + NG))(
                functools.partial(stage, t - number)
            )
        return carry

    lax.fori_loop(0, NG + len(stages) - 1, step, 0)
    returned[my_rows(me), :] = summed[my_rows(me), :]

    slots = (NSEQ - 1) * CAP
    remote(
        returned.at[0:slots], returned.at[0:slots], s_ret, r_ret, seq=me
    ).wait_recv()
    for c in range(PART // HD):
        lanes = slice(c * HD, (c + 1) * HD)
        out_ref[:, lanes] = (
            middle[:, lanes].astype(F32)
            + (
                nn(picks[0], returned[:, lanes]) * mixes[0]
                + nn(picks[1], returned[:, lanes]) * mixes[1]
            )
        ).astype(BF16)

    remote(
        outgoing.at[0 : NSEQ - 1], outgoing.at[0 : NSEQ - 1], s_disp, r_disp.at[0], seq=me
    ).wait_send()
    remote(
        rows_in.at[0 : NX - 1], rows_in.at[0 : NX - 1], s_gath, r_gath.at[0, 0], head=hd
    ).wait_send()
    remote(rows_in.at[0:NX], rows_in.at[0:NX], s_fwd, r_fwd.at[0], head=hd).wait_send()
    remote(pair_in, pair_in, s_pair, r_pair.at[0], head=hd).wait_send()
    remote(far_sum, far_sum, s_ring, r_ring.at[0, 0], head=hd).wait_send()
    remote(plane_in, plane_in, s_plane, r_plane.at[0], head=hd).wait_send()
    remote(
        returned.at[0:slots], returned.at[0:slots], s_ret, r_ret, seq=me
    ).wait_send()
    remote(
        own_state.at[0:others], all_state.at[0:others], s_state, r_state, seq=me
    ).wait_send()
    remote(
        all_info.at[0:others], all_info.at[0:others], s_info, r_info, seq=me
    ).wait_send()
    remote(
        own_carry.at[0:others], all_carry.at[0:others], s_carry, r_carry, seq=me
    ).wait_send()
    remote(attended.at[0:3], attended.at[0:3], s_att, r_att.at[0, 0], seq=me).wait_send()
    w_copy(pl.ds(0, (NZ - 1) * WCOLS), 0, me, 0).wait_send()
    remote(paired, paired, s_pp, r_pp.at[0], head=hd).wait_send()
    remote(
        arrived.at[:, 0 : NX - 1],
        arrived.at[:, 0 : NX - 1],
        s_part,
        r_part.at[0],
        head=hd,
    ).wait_send()
    remote(
        column_in.at[0 : NY - 1], column_in.at[0 : NY - 1], s_col, r_col, seq=me
    ).wait_send()


def layer(*operands):
    vmem = pl.BlockSpec(memory_space=pltpu.VMEM)
    anywhere = pl.BlockSpec(memory_space=pl.ANY)
    dma = pltpu.SemaphoreType.DMA
    return pl.pallas_call(
        layer_kernel,
        out_shape=jax.ShapeDtypeStruct((TOK, PART), BF16),
        in_specs=[vmem] * 11 + [anywhere] * 3,
        out_specs=vmem,
        scratch_shapes=[
            pltpu.VMEM((HEADS, TOK), F32),
            pltpu.VMEM((NSEQ, 32, HD), BF16),
            pltpu.VMEM((HEADS, 1, TOK), F32),
            pltpu.VMEM((NSEQ, 32, HD), BF16),
            pltpu.VMEM((NSEQ, 1, TOK), F32),
            pltpu.VMEM((NSEQ, 32, HD), BF16),
            pltpu.VMEM((NSEQ, 32, HD), BF16),
            pltpu.VMEM((TOK, HEADS * HD), F32),
            pltpu.VMEM((NY, TOK, HEADS * HD), BF16),
            pltpu.VMEM((NZ * WCOLS, HEADS * HD), BF16),
            pltpu.VMEM((NY, NX, 2, WCOLS, TOK), BF16),
            pltpu.VMEM((NY, NX, WCOLS, TOK), BF16),
            pltpu.VMEM((NY, NX, WCOLS, TOK), BF16),
            pltpu.VMEM((NY, NX, WCOLS, TOK), BF16),
            pltpu.VMEM((NY, WCOLS, TOK), BF16),
            pltpu.VMEM((NY, WCOLS, TOK), BF16),
            pltpu.VMEM((TOK, PART), BF16),
            pltpu.VMEM((SLOTS, TOK), BF16),
            pltpu.VMEM((2, TOK, SLOTS), BF16),
            pltpu.VMEM((2, TOK, TOK), F32),
            pltpu.VMEM((FF, D), BF16),
            pltpu.VMEM((FF, D), BF16),
            pltpu.VMEM((FF, D), BF16),
            pltpu.VMEM((NSEQ, CAP, PART), BF16),
            pltpu.VMEM((NHEAD, SLOTS, PART), BF16),
            pltpu.VMEM((GROWS, D), BF16),
            pltpu.VMEM((2, NX, SLOTS, PART), BF16),
            pltpu.VMEM((NX, SLOTS, PART), BF16),
            pltpu.VMEM((SLOTS, PART), BF16),
            pltpu.VMEM((SLOTS, PART), BF16),
            pltpu.VMEM((2, SLOTS, PART), BF16),
            pltpu.VMEM((2, SLOTS, PART), BF16),
            pltpu.VMEM((SLOTS, PART), BF16),
            pltpu.VMEM((SLOTS, PART), BF16),
            dma,
            dma,
            dma,
            dma,
            dma,
            dma,
            dma,
            dma((3, 2)),
            dma,
            dma((2, 4)),
            dma,
            dma((NY,)),
            dma,
            dma((NY,)),
            dma,
            dma,
            dma((3,)),
            dma,
            dma((NG,)),
            dma,
            dma((NG, 4)),
            dma,
            dma((NG,)),
            dma,
            dma((NG,)),
            dma,
            dma((NG, 2)),
            dma,
            dma((NG,)),
            dma,
            dma,
        ],
        compiler_params=pltpu.CompilerParams(
            collective_id=0, has_side_effects=True, vmem_limit_bytes=VMEM_LIMIT
        ),
        name="layer",
    )(*operands)


def shards(
    queries,
    key_vectors,
    value_vectors,
    log_decay,
    doc_ids,
    head_gain,
    output_weight,
    residual,
    norm_gain,
    routing,
    route_weights,
    gate_weight,
    up_weight,
    down_weight,
):
    return layer(
        queries,
        key_vectors,
        value_vectors,
        log_decay.T,
        doc_ids.reshape(1, -1),
        head_gain.reshape(1, -1),
        output_weight.T,
        residual,
        routing.T,
        route_weights.T,
        norm_gain.reshape(1, -1),
        gate_weight[0].T,
        up_weight[0].T,
        down_weight[0],
    )


def solution(mesh):
    in_specs = (
        P("seq", "head"),
        P("seq", "head"),
        P("seq", "head"),
        P("seq", "head"),
        P("seq"),
        P("head"),
        P("head", "seq"),
        P("seq", "head"),
        P(),
        P("seq", None),
        P("seq", None),
        P("seq", None, "head"),
        P("seq", None, "head"),
        P("seq", "head", None),
    )
    return jax.shard_map(
        shards, mesh=mesh, in_specs=in_specs, out_specs=P("seq", "head"), check_vma=False
    )
```

time: 123 us -> 116 us (0.943)
  Pallas kernels: 120 us -> 113 us
    pallas_call x2 -> x1, Pallas kernels: 120 us -> 113 us  [layer(): pl.pallas_call(layer_kernel, out_shape=jax.ShapeDtypeStruct((TOK, PART),...]
where the time goes in v3:
time: 116 us; the launch traced here: 115 us
  Pallas kernels  113 us (97%)
  local copies, waits for them, and re-layouts  1.54 us (1%)
    pallas_call x1, Pallas kernels, layer(): pl.pallas_call(layer_kernel, out_shape=jax.ShapeDtypeStruct((TOK, PART),...  113 us

profile of v3, /device:TPU:2, one launch (start us, length us, event | category | flops | bytes accessed | tf_op | source)
XLA Modules:
  0.0 114.8 jit_solution(12379030487488949494)
XLA Ops:
  0.0 113.2 %layer.1 = bf16[128,384]{1,0:T(8,128)(2,1)} custom-call(bf16[128,1024]{1,0:T(8,128)(2,1)} %q_ref.1, bf16[128,1024]{1,0:T(8,128)(2,1)} %k_ref.1, bf16[128,1024]{1,0:T(8,128)(2,1)} %v_ref.1, f32[8,128]{1,0:T(8,128)} %bitcast.19, s32[1,128]{1,0:T(1,128)} %bitcast.23, f32[1,1024]{1,0:T(1,128)} %bitcast.20, bf16[96,1024]{1,0:T(8,128)(2,1)} %bitcast.17, ...), custom_call_target="tpu_custom_call" | custom-call | tf_op jit(solution)/shard_map/layer/pallas_call | solution.py:645
  113.2 1.5 %copy.16 = bf16[128,384]{1,0:T(8,128)(2,1)} copy(bf16[128,384]{1,0:T(8,128)(2,1)} %layer.1) | data formatting | bytes 196608

commit v4 on v3

--- a/solution.py
+++ b/solution.py
@@ -66,27 +66,42 @@
     return i + i // 2 - 2 * (i // 3)
 
 
+def around(n):
+    return (n + 1) // 2 * (2 * lax.rem(n, 2) - 1)
+
+
 def columns(row):
     return jnp.transpose(jnp.broadcast_to(row, (TOK, TOK)))
 
 
 def layer_kernel(
+    q_hbm,
+    k_hbm,
+    v_hbm,
+    ld_hbm,
+    doc_hbm,
+    hg_hbm,
+    w_hbm,
+    res_hbm,
+    rout_hbm,
+    mix_hbm,
+    ng_hbm,
+    gate_hbm,
+    up_hbm,
+    down_hbm,
+    out_ref,
     q_ref,
     k_ref,
     v_ref,
     ld_ref,
     doc_ref,
     hg_ref,
-    w_ref,
     res_ref,
     rout_ref,
     mix_ref,
     ng_ref,
-    gate_hbm,
-    up_hbm,
-    down_hbm,
-    out_ref,
     decay,
+    reaches,
     own_state,
     own_info,
     all_state,
@@ -137,6 +152,7 @@
     s_col,
     r_col,
     s_load,
+    s_in,
     s_disp,
     r_disp,
     s_gath,
@@ -163,8 +179,34 @@
         pltpu.make_async_copy(up_hbm, up, s_load.at[1]),
         pltpu.make_async_copy(down_hbm, down, s_load.at[2]),
     ]
+
+    def w_rows(z, start=0, size=WCOLS):
+        return pl.ds(pl.multiple_of(lax.rem(z + NZ, NZ) * WCOLS + start, 16), size)
+
+    fetches = [
+        pltpu.make_async_copy(source, target, s_in.at[n])
+        for n, (source, target) in enumerate(
+            (
+                (ld_hbm, ld_ref),
+                (doc_hbm, doc_ref),
+                (k_hbm, k_ref),
+                (v_hbm, v_ref),
+                (w_hbm, weight.at[w_rows(zi)]),
+                (q_hbm, q_ref),
+                (rout_hbm, rout_ref),
+                (mix_hbm, mix_ref),
+                (hg_hbm, hg_ref),
+                (res_hbm, res_ref),
+                (ng_hbm, ng_ref),
+            )
+        )
+    ]
+    for fetch in fetches:
+        fetch.start()
     for load in loads:
         load.start()
+    for fetch in fetches[0:4]:
+        fetch.wait()
 
     rows = lax.broadcasted_iota(jnp.int32, (TOK, TOK), 0)
     cols = lax.broadcasted_iota(jnp.int32, (TOK, TOK), 1)
@@ -191,16 +233,13 @@
     pl.semaphore_wait(barrier, NSEQ + NHEAD - 2)
 
     @pl.loop(1, NSEQ)
-    def _(d):
-        to = lax.rem(me + d, NSEQ)
+    def _(n):
+        to = lax.rem(me + NSEQ + around(n), NSEQ)
         remote(own_info.at[to // 4], all_info.at[me], s_info, r_info, seq=to).start()
         remote(own_state.at[to], all_state.at[me], s_state, r_state, seq=to).start()
 
     all_state[me] = own_state[me]
     all_info[me] = own_info[me // 4]
-
-    def w_rows(z, start=0, size=WCOLS):
-        return pl.ds(pl.multiple_of(lax.rem(z + NZ, NZ) * WCOLS + start, 16), size)
 
     right = lax.rem(zi + 1, NZ) * NY + yi
     left = lax.rem(zi + NZ - 1, NZ) * NY + yi
@@ -218,8 +257,11 @@
         from_right = w_rows(zi + 1 + k) if k < 2 else w_rows(zi + 1 + k, half, half)
         w_copy(from_right, k + 1, left, 1).start()
 
-    remote(w_ref, weight.at[w_rows(zi)], s_w, r_w.at[0, 0], seq=right).start()
-    remote(w_ref, weight.at[w_rows(zi)], s_w, r_w.at[1, 0], seq=left).start()
+    fetches[4].wait()
+    w_copy(w_rows(zi), 0, right, 0).start()
+    w_copy(w_rows(zi), 0, left, 1).start()
+    for fetch in fetches[5:]:
+        fetch.wait()
 
     doc_rows = jnp.broadcast_to(doc, (TOK, TOK))
     kept = (cols <= rows) & (jnp.transpose(doc_rows) == doc_rows)
@@ -230,7 +272,6 @@
         factor = jnp.where(kept, jnp.exp(jnp.minimum(gap, 0.0)), 0.0)
         weighted = (nt(q_ref[:, lanes], k_ref[:, lanes]) * factor).astype(BF16)
         inner[:, lanes] = nn(weighted, v_ref[:, lanes])
-    weight[w_rows(zi), :] = w_ref[...]
     expert = lax.broadcasted_iota(jnp.int32, (NSEQ, TOK), 0)
     hits = [(expert == rout_ref[j : j + 1, :]).astype(F32) for j in range(2)]
     earlier = (
@@ -260,61 +301,64 @@
         all_info.at[0:others], all_info.at[0:others], s_info, r_info, seq=me
     ).wait_recv()
 
-    def scan(b, carry):
-        carried, before = carry
+    carried, before = jnp.zeros((32, HD), F32), jnp.full((1, 1), -1.0, F32)
+    for b in range(NSEQ):
         own_carry[b] = carried.astype(BF16)
         row = all_info[b]
         through = jnp.where(row[:, 32:33] == before, row[:, 0:1], 0.0)
-        return all_state[b].astype(F32) + through * carried, row[:, 64:65]
-
-    lax.fori_loop(
-        0,
-        NSEQ,
-        scan,
-        (jnp.zeros((32, HD), F32), jnp.full((1, 1), -1.0, F32)),
-        unroll=4,
-    )
+        carried, before = all_state[b].astype(F32) + through * carried, row[:, 64:65]
 
     @pl.loop(1, NSEQ)
-    def _(d):
-        to = lax.rem(me + d, NSEQ)
-        remote(own_carry.at[to], all_carry.at[me], s_carry, r_carry, seq=to).start()
+    def _(n):
+        to = lax.rem(me + NSEQ + around(n), NSEQ)
+        remote(
+            own_carry.at[to], all_carry.at[me], s_carry, r_carry.at[me // 16], seq=to
+        ).start()
 
     all_carry[me] = own_carry[me]
     before_doc = all_info[jnp.maximum(me - 1, 0)][:, 64:65]
     before_doc = jnp.where(jnp.full((1, 1), me, jnp.int32) == 0, -1.0, before_doc)
     w_step(0)
-    reach = jnp.exp(decay[...]) * (doc == before_doc).astype(F32)
-    remote(
-        own_carry.at[0:others], all_carry.at[0:others], s_carry, r_carry, seq=me
-    ).wait_recv()
-    w_step(1)
+    reaches[...] = jnp.exp(decay[...]) * (doc == before_doc).astype(F32)
     y_up = zi * NY + lax.rem(yi + 1, NY)
     y_down = zi * NY + lax.rem(yi + NY - 1, NY)
+    near = me // 16
+
+    def half_lanes(part):
+        return pl.ds(pl.multiple_of(part * 512, 512), 512)
 
     def att_half(y, part):
-        return attended.at[lax.rem(y + NY, NY), :, part * 512 : (part + 1) * 512]
+        return attended.at[lax.rem(y + NY, NY), :, half_lanes(part)]
 
     def att_wait(block, side, part):
         remote(block, block, s_att, r_att.at[side, part], seq=me).wait_recv()
 
-    for h in range(HEADS):
-        lanes = slice(h * HD, (h + 1) * HD)
-        carried = all_carry[4 * h : 4 * h + 4].reshape(HD, HD)
-        raw = inner[:, lanes] + nn(q_ref[:, lanes], carried) * columns(reach[h : h + 1, :])
-        scale = lax.rsqrt(jnp.mean(raw * raw, axis=1, keepdims=True) + EPSILON)
-        attended[yi, :, lanes] = (raw * scale * hg_ref[:, lanes]).astype(BF16)
-        if h % 2 == 1:
-            pair = slice((h - 1) * HD, (h + 1) * HD)
-            block = attended.at[yi, :, pair]
-            remote(block, block, s_att, r_att.at[0, h // 4], seq=y_up).start()
-            remote(block, block, s_att, r_att.at[1, h // 4], seq=y_down).start()
-
-    block = att_half(yi - 1, 0)
+    for order in range(2):
+        part = near if order == 0 else 1 - near
+        slabs = own_carry.at[0 : 15 if order == 0 else 16]
+        remote(slabs, slabs, s_carry, r_carry.at[part], seq=me).wait_recv()
+        for j in range(4):
+            h = part * 4 + j
+            lanes = pl.ds(pl.multiple_of(h * HD, HD), HD)
+            carried = all_carry[pl.ds(4 * h, 4)].reshape(HD, HD)
+            raw = inner[:, lanes] + nn(q_ref[:, lanes], carried) * columns(
+                reaches[pl.ds(h, 1), :]
+            )
+            scale = lax.rsqrt(jnp.mean(raw * raw, axis=1, keepdims=True) + EPSILON)
+            attended[yi, :, lanes] = (raw * scale * hg_ref[:, lanes]).astype(BF16)
+            if j % 2 == 1:
+                pair = pl.ds(pl.multiple_of((h - 1) * HD, 2 * HD), 2 * HD)
+                block = attended.at[yi, :, pair]
+                remote(block, block, s_att, r_att.at[0, order], seq=y_up).start()
+                remote(block, block, s_att, r_att.at[1, order], seq=y_down).start()
+        if order == 0:
+            w_step(1)
+
+    block = att_half(yi - 1, near)
     att_wait(block, 0, 0)
     remote(block, block, s_att, r_att.at[2, 0], seq=y_up).start()
     w_step(2)
-    block = att_half(yi + 1, 1)
+    block = att_half(yi + 1, 1 - near)
     att_wait(block, 1, 1)
     remote(block, block, s_att, r_att.at[2, 1], seq=y_down).start()
     w_copy(w_rows(zi + 4, 0, half), 3, me, 0).wait_recv()
@@ -322,13 +366,13 @@
 
     def project(i):
         y = lax.rem(yi + NY - turn(i), NY)
-        pl.when(i == 1)(lambda: att_wait(att_half(yi - 1, 1), 0, 1))
-        pl.when(i == 2)(lambda: att_wait(att_half(yi + 1, 0), 1, 0))
+        pl.when(i == 1)(lambda: att_wait(att_half(yi - 1, 1 - near), 0, 1))
+        pl.when(i == 2)(lambda: att_wait(att_half(yi + 1, near), 1, 0))
 
         @pl.when(i == 3)
         def _():
-            att_wait(att_half(yi + 2, 0), 2, 0)
-            att_wait(att_half(yi + 2, 1), 2, 1)
+            att_wait(att_half(yi + 2, near), 2, 0)
+            att_wait(att_half(yi + 2, 1 - near), 2, 1)
 
         partial[y] = nt(weight[...], attended[y]).astype(BF16).reshape(NX, 2, WCOLS, TOK)
         remote(
@@ -381,11 +425,11 @@
 
     def project_step(t, carry):
         pl.when(t < NY)(lambda: project(t))
-        pl.when((t >= 1) & (t < NY + 1))(lambda: pair_sum(t - 1))
-        pl.when(t >= 2)(lambda: plane_sum(t - 2))
+        pl.when(t >= 1)(lambda: pair_sum(t - 1))
         return carry
 
-    lax.fori_loop(0, NY + 2, project_step, 0)
+    lax.fori_loop(0, NY + 1, project_step, 0)
+    pl.loop(0, NY)(plane_sum)
     remote(
         column_in.at[0 : NY - 1], column_in.at[0 : NY - 1], s_col, r_col, seq=me
     ).wait_recv()
@@ -429,22 +473,8 @@
         g = lax.rem(group + NG - turn(i), NG)
         part = group_rows(g)
 
-        @pl.when(i == 0)
-        def _():
-            remote(
-                outgoing.at[0 : GSRC - 1],
-                outgoing.at[0 : GSRC - 1],
-                s_disp,
-                r_disp.at[g],
-                seq=me,
-            ).wait_recv()
-
-        @pl.when(i > 0)
-        def _():
-            remote(
-                outgoing.at[0:GSRC], outgoing.at[0:GSRC], s_disp, r_disp.at[g], seq=me
-            ).wait_recv()
-
+        blocks = outgoing.at[0 : GSRC - 1 if i == 0 else GSRC]
+        remote(blocks, blocks, s_disp, r_disp.at[g], seq=me).wait_recv()
         block = rows_in.at[hd, part]
         remote(block, block, s_gath, r_gath.at[g, 0], head=x_up).start()
         remote(block, block, s_gath, r_gath.at[g, 1], head=x_down).start()
@@ -472,11 +502,9 @@
         g = lax.rem(group + NG - turn(i), NG)
         part = group_rows(g)
 
-        @pl.when(i == 0)
-        def _():
+        if i == 0:
             for load in loads:
                 load.wait()
-
         remote(
             rows_in.at[0:NX, 0:GROWS], rows_in.at[0:NX, 0:GROWS], s_fwd, r_fwd.at[g], head=hd
         ).wait_recv()
@@ -567,24 +595,37 @@
                     summed.at[my_rows(to)], returned.at[my_rows(me)], s_ret, r_ret, seq=to
                 ).start()
 
-    stages = (
-        gather,
-        forward,
-        forward_far,
-        serve,
-        reduce_pair,
-        reduce_mid,
-        reduce_plane,
-    )
-
-    def step(t, carry):
-        for number, stage in enumerate(stages):
-            pl.when((t >= number) & (t < number + NG))(
-                functools.partial(stage, t - number)
-            )
-        return carry
-
-    lax.fori_loop(0, NG + len(stages) - 1, step, 0)
+    for stage, i in (
+        (gather, 0),
+        (gather, 1),
+        (forward, 0),
+        (gather, 2),
+        (forward, 1),
+        (forward_far, 0),
+        (gather, 3),
+        (serve, 0),
+        (forward, 2),
+        (forward_far, 1),
+        (forward, 3),
+        (serve, 1),
+        (reduce_pair, 0),
+        (forward_far, 2),
+        (forward_far, 3),
+        (serve, 2),
+        (reduce_pair, 1),
+        (reduce_mid, 0),
+        (serve, 3),
+        (reduce_pair, 2),
+        (reduce_mid, 1),
+        (reduce_pair, 3),
+        (reduce_plane, 0),
+        (reduce_mid, 2),
+        (reduce_plane, 1),
+        (reduce_mid, 3),
+        (reduce_plane, 2),
+        (reduce_plane, 3),
+    ):
+        stage(i)
     returned[my_rows(me), :] = summed[my_rows(me), :]
 
     slots = (NSEQ - 1) * CAP
@@ -621,7 +662,7 @@
         all_info.at[0:others], all_info.at[0:others], s_info, r_info, seq=me
     ).wait_send()
     remote(
-        own_carry.at[0:others], all_carry.at[0:others], s_carry, r_carry, seq=me
+        own_carry.at[0:others], all_carry.at[0:others], s_carry, r_carry.at[0], seq=me
     ).wait_send()
     remote(attended.at[0:3], attended.at[0:3], s_att, r_att.at[0, 0], seq=me).wait_send()
     w_copy(pl.ds(0, (NZ - 1) * WCOLS), 0, me, 0).wait_send()
@@ -645,9 +686,20 @@
     return pl.pallas_call(
         layer_kernel,
         out_shape=jax.ShapeDtypeStruct((TOK, PART), BF16),
-        in_specs=[vmem] * 11 + [anywhere] * 3,
+        in_specs=[anywhere] * 14,
         out_specs=vmem,
         scratch_shapes=[
+            pltpu.VMEM((TOK, HEADS * HD), BF16),
+            pltpu.VMEM((TOK, HEADS * HD), BF16),
+            pltpu.VMEM((TOK, HEADS * HD), BF16),
+            pltpu.VMEM((HEADS, TOK), F32),
+            pltpu.VMEM((1, TOK), jnp.int32),
+            pltpu.VMEM((1, HEADS * HD), F32),
+            pltpu.VMEM((TOK, PART), BF16),
+            pltpu.VMEM((2, TOK), jnp.int32),
+            pltpu.VMEM((2, TOK), F32),
+            pltpu.VMEM((1, D), F32),
+            pltpu.VMEM((HEADS, TOK), F32),
             pltpu.VMEM((HEADS, TOK), F32),
             pltpu.VMEM((NSEQ, 32, HD), BF16),
             pltpu.VMEM((HEADS, 1, TOK), F32),
@@ -687,7 +739,7 @@
             dma,
             dma,
             dma,
-            dma,
+            dma((2,)),
             dma,
             dma((3, 2)),
             dma,
@@ -699,6 +751,7 @@
             dma,
             dma,
             dma((3,)),
+            dma((11,)),
             dma,
             dma((NG,)),
             dma,

time: 116 us -> 115 us (level)
  Pallas kernels: 113 us -> 111 us
    pallas_call x1, Pallas kernels: 113 us -> 111 us  [layer(): pl.pallas_call(layer_kernel, out_shape=jax.ShapeDtypeStruct((TOK, PART),...]
where the time goes in v4:
time: 115 us; the launch traced here: 113 us
  Pallas kernels  111 us (97%)
  local copies, waits for them, and re-layouts  1.54 us (1%)
    pallas_call x1, Pallas kernels, layer(): pl.pallas_call(layer_kernel, out_shape=jax.ShapeDtypeStruct((TOK, PART),...  111 us

profile of v4, /device:TPU:2, one launch (start us, length us, event | category | flops | bytes accessed | tf_op | source)
XLA Modules:
  0.0 112.9 jit_solution(450263905022395946)
XLA Ops:
  0.0 111.3 %layer.1 = bf16[128,384]{1,0:T(8,128)(2,1)} custom-call(bf16[128,1024]{1,0:T(8,128)(2,1)} %q_hbm.1, bf16[128,1024]{1,0:T(8,128)(2,1)} %k_hbm.1, bf16[128,1024]{1,0:T(8,128)(2,1)} %v_hbm.1, f32[8,128]{1,0:T(8,128)} %bitcast.19, s32[1,128]{1,0:T(1,128)} %bitcast.23, f32[1,1024]{1,0:T(1,128)} %bitcast.20, bf16[96,1024]{1,0:T(8,128)(2,1)} %bitcast.17, ...), custom_call_target="tpu_custom_call" | custom-call | tf_op jit(solution)/shard_map/layer/pallas_call | solution.py:686
  111.3 1.5 %copy.16 = bf16[128,384]{1,0:T(8,128)(2,1)} copy(bf16[128,384]{1,0:T(8,128)(2,1)} %layer.1) | data formatting | bytes 196608

commit v5 on v4

--- a/solution.py
+++ b/solution.py
@@ -127,6 +127,7 @@
     outgoing,
     rows_in,
     normed,
+    hidden,
     result,
     pair_in,
     far_sum,
@@ -456,9 +457,10 @@
     def group_rows(index):
         return pl.ds(pl.multiple_of(index * GROWS, GROWS), GROWS)
 
-    @pl.loop(1, NSEQ)
+    @pl.loop(0, NSEQ - 1)
     def _(n):
-        to = lax.rem(group + turn(n // GSRC), NG) * GSRC + lax.rem(me + n, GSRC)
+        n = n + n // (NSEQ - GSRC)
+        to = lax.rem(group + 1 + n // GSRC, NG) * GSRC + lax.rem(me + n, GSRC)
         remote(
             outgoing.at[to],
             rows_in.at[hd, my_rows(me)],
@@ -469,11 +471,14 @@
 
     rows_in[hd, my_rows(me), :] = outgoing[me]
 
+    def source_group(i):
+        return lax.rem(group + NG - 1 - i, NG)
+
     def gather(i):
-        g = lax.rem(group + NG - turn(i), NG)
+        g = source_group(i)
         part = group_rows(g)
 
-        blocks = outgoing.at[0 : GSRC - 1 if i == 0 else GSRC]
+        blocks = outgoing.at[0 : GSRC - 1 if i == NG - 1 else GSRC]
         remote(blocks, blocks, s_disp, r_disp.at[g], seq=me).wait_recv()
         block = rows_in.at[hd, part]
         remote(block, block, s_gath, r_gath.at[g, 0], head=x_up).start()
@@ -481,7 +486,7 @@
         remote(block, block, s_fwd, r_fwd.at[g], head=partner).start()
 
     def forward(i):
-        g = lax.rem(group + NG - turn(i), NG)
+        g = source_group(i)
         part = group_rows(g)
         for side, source, to in ((0, x_down, x_up), (1, x_up, x_down)):
             block = rows_in.at[source, part]
@@ -491,54 +496,68 @@
             remote(block, block, s_fwd, r_fwd.at[g], head=partner).start()
 
     def forward_far(i):
-        g = lax.rem(group + NG - turn(i), NG)
+        g = source_group(i)
         for side in range(2):
             piece = rows_in.at[x_far, half_rows(g, side)]
             remote(piece, piece, s_gath, r_gath.at[g, 2 + side], head=hd).wait_recv()
         block = rows_in.at[x_far, group_rows(g)]
         remote(block, block, s_fwd, r_fwd.at[g], head=partner).start()
 
-    def serve(i):
-        g = lax.rem(group + NG - turn(i), NG)
-        part = group_rows(g)
-
-        if i == 0:
+    def serve_up(pair):
+        if pair == 0:
             for load in loads:
                 load.wait()
-        remote(
-            rows_in.at[0:NX, 0:GROWS], rows_in.at[0:NX, 0:GROWS], s_fwd, r_fwd.at[g], head=hd
-        ).wait_recv()
-        squares = jnp.zeros((GROWS, HD), F32)
-        for h in range(NHEAD):
-            block = rows_in[h, part, :].astype(F32)
-            block = block * block
-            for c in range(PART // HD):
-                squares = squares + block[:, c * HD : (c + 1) * HD]
-        scale = lax.rsqrt(jnp.sum(squares, axis=1, keepdims=True) / D + EPSILON)
+        for n in range(2):
+            g = source_group(2 * pair + n)
+            part = group_rows(g)
+            target = slice(n * GROWS, (n + 1) * GROWS)
+            remote(
+                rows_in.at[0:NX, 0:GROWS],
+                rows_in.at[0:NX, 0:GROWS],
+                s_fwd,
+                r_fwd.at[g],
+                head=hd,
+            ).wait_recv()
+            squares = jnp.zeros((GROWS, HD), F32)
+            for h in range(NHEAD):
+                block = rows_in[h, part, :].astype(F32)
+                block = block * block
+                for c in range(PART // HD):
+                    squares = squares + block[:, c * HD : (c + 1) * HD]
+            scale = lax.rsqrt(jnp.sum(squares, axis=1, keepdims=True) / D + EPSILON)
+            for h in range(NHEAD):
+                lanes = slice(h * PART, (h + 1) * PART)
+                normed[target, lanes] = (
+                    rows_in[h, part, :].astype(F32) * scale * ng_ref[:, lanes]
+                ).astype(BF16)
+        gated = nt(normed[...], gate[...])
+        upped = nt(normed[...], up[...])
+        hidden[...] = (gated / (1.0 + jnp.exp(-gated)) * upped).astype(BF16)
+
+    def serve_down(pair):
+        groups = [source_group(2 * pair + n) for n in range(2)]
         for h in range(NHEAD):
             lanes = slice(h * PART, (h + 1) * PART)
-            normed[:, lanes] = (
-                rows_in[h, part, :].astype(F32) * scale * ng_ref[:, lanes]
-            ).astype(BF16)
-        gated = nt(normed[...], gate[...])
-        upped = nt(normed[...], up[...])
-        hidden = (gated / (1.0 + jnp.exp(-gated)) * upped).astype(BF16)
-        for h in range(NHEAD):
-            lanes = slice(h * PART, (h + 1) * PART)
-            result[h % 2, h // 2, part, :] = nn(hidden, down[:, lanes]).astype(BF16)
-        remote(
-            result.at[1 - core, :, part],
-            pair_in.at[:, part],
-            s_pair,
-            r_pair.at[g],
-            head=partner,
-        ).start()
+            product = nn(hidden[...], down[:, lanes]).astype(BF16)
+            for n, g in enumerate(groups):
+                result[h % 2, h // 2, group_rows(g), :] = product[
+                    n * GROWS : (n + 1) * GROWS
+                ]
+        for g in groups:
+            part = group_rows(g)
+            remote(
+                result.at[1 - core, :, part],
+                pair_in.at[:, part],
+                s_pair,
+                r_pair.at[g],
+                head=partner,
+            ).start()
 
     def both_cores(x, rows):
         return result[core, x, rows, :].astype(F32) + pair_in[x, rows, :].astype(F32)
 
     def reduce_pair(i):
-        g = lax.rem(group + NG - turn(i), NG)
+        g = source_group(i)
         part = group_rows(g)
         remote(
             pair_in.at[:, part], pair_in.at[:, part], s_pair, r_pair.at[g], head=hd
@@ -555,7 +574,7 @@
             ).start()
 
     def reduce_mid(i):
-        g = lax.rem(group + NG - turn(i), NG)
+        g = source_group(i)
         part = group_rows(g)
         for side, to in ((0, x_up), (1, x_down)):
             piece, other = half_rows(g, side), half_rows(g, 1 - side)
@@ -575,7 +594,7 @@
             ).start()
 
     def reduce_plane(i):
-        g = lax.rem(group + NG - turn(i), NG)
+        g = source_group(i)
         part = group_rows(g)
         remote(
             plane_in.at[:, part], plane_in.at[:, part], s_plane, r_plane.at[g], head=hd
@@ -601,26 +620,26 @@
         (forward, 0),
         (gather, 2),
         (forward, 1),
+        (gather, 3),
         (forward_far, 0),
-        (gather, 3),
-        (serve, 0),
+        (forward_far, 1),
         (forward, 2),
-        (forward_far, 1),
+        (serve_up, 0),
         (forward, 3),
-        (serve, 1),
+        (serve_down, 0),
+        (forward_far, 2),
         (reduce_pair, 0),
-        (forward_far, 2),
+        (reduce_pair, 1),
         (forward_far, 3),
-        (serve, 2),
-        (reduce_pair, 1),
+        (serve_up, 1),
         (reduce_mid, 0),
-        (serve, 3),
+        (reduce_mid, 1),
+        (serve_down, 1),
         (reduce_pair, 2),
-        (reduce_mid, 1),
+        (reduce_plane, 0),
         (reduce_pair, 3),
-        (reduce_plane, 0),
+        (reduce_plane, 1),
         (reduce_mid, 2),
-        (reduce_plane, 1),
         (reduce_mid, 3),
         (reduce_plane, 2),
         (reduce_plane, 3),
@@ -725,7 +744,8 @@
             pltpu.VMEM((FF, D), BF16),
             pltpu.VMEM((NSEQ, CAP, PART), BF16),
             pltpu.VMEM((NHEAD, SLOTS, PART), BF16),
-            pltpu.VMEM((GROWS, D), BF16),
+            pltpu.VMEM((2 * GROWS, D), BF16),
+            pltpu.VMEM((2 * GROWS, FF), BF16),
             pltpu.VMEM((2, NX, SLOTS, PART), BF16),
             pltpu.VMEM((NX, SLOTS, PART), BF16),
             pltpu.VMEM((SLOTS, PART), BF16),

time: 115 us -> 109 us (0.948)
  Pallas kernels: 111 us -> 106 us
    pallas_call x1, Pallas kernels: 111 us -> 106 us  [layer(): pl.pallas_call(layer_kernel, out_shape=jax.ShapeDtypeStruct((TOK, PART),...]
where the time goes in v5:
time: 109 us; the launch traced here: 108 us
  Pallas kernels  106 us (97%)
  local copies, waits for them, and re-layouts  1.54 us (1%)
    pallas_call x1, Pallas kernels, layer(): pl.pallas_call(layer_kernel, out_shape=jax.ShapeDtypeStruct((TOK, PART),...  106 us

profile of v5, /device:TPU:2, one launch (start us, length us, event | category | flops | bytes accessed | tf_op | source)
XLA Modules:
  0.0 107.6 jit_solution(1519389920983592533)
XLA Ops:
  0.0 106.0 %layer.1 = bf16[128,384]{1,0:T(8,128)(2,1)} custom-call(bf16[128,1024]{1,0:T(8,128)(2,1)} %q_hbm.1, bf16[128,1024]{1,0:T(8,128)(2,1)} %k_hbm.1, bf16[128,1024]{1,0:T(8,128)(2,1)} %v_hbm.1, f32[8,128]{1,0:T(8,128)} %bitcast.19, s32[1,128]{1,0:T(1,128)} %bitcast.23, f32[1,1024]{1,0:T(1,128)} %bitcast.20, bf16[96,1024]{1,0:T(8,128)(2,1)} %bitcast.17, ...), custom_call_target="tpu_custom_call" | custom-call | tf_op jit(solution)/shard_map/layer/pallas_call | solution.py:705
  106.0 1.5 %copy.16 = bf16[128,384]{1,0:T(8,128)(2,1)} copy(bf16[128,384]{1,0:T(8,128)(2,1)} %layer.1) | data formatting | bytes 196608

commit v6 on v5

--- a/solution.py
+++ b/solution.py
@@ -64,10 +64,6 @@
 
 def turn(i):
     return i + i // 2 - 2 * (i // 3)
-
-
-def around(n):
-    return (n + 1) // 2 * (2 * lax.rem(n, 2) - 1)
 
 
 def columns(row):
@@ -235,7 +231,7 @@
 
     @pl.loop(1, NSEQ)
     def _(n):
-        to = lax.rem(me + NSEQ + around(n), NSEQ)
+        to = lax.rem(me + n, NSEQ)
         remote(own_info.at[to // 4], all_info.at[me], s_info, r_info, seq=to).start()
         remote(own_state.at[to], all_state.at[me], s_state, r_state, seq=to).start()
 
@@ -311,7 +307,7 @@
 
     @pl.loop(1, NSEQ)
     def _(n):
-        to = lax.rem(me + NSEQ + around(n), NSEQ)
+        to = lax.rem(me + n, NSEQ)
         remote(
             own_carry.at[to], all_carry.at[me], s_carry, r_carry.at[me // 16], seq=to
         ).start()
@@ -636,8 +632,8 @@
         (reduce_mid, 1),
         (serve_down, 1),
         (reduce_pair, 2),
+        (reduce_pair, 3),
         (reduce_plane, 0),
-        (reduce_pair, 3),
         (reduce_plane, 1),
         (reduce_mid, 2),
         (reduce_mid, 3),

time: 109 us -> 110 us (level)
  no operation moved by 1% of the time
where the time goes in v6:
time: 110 us; the launch traced here: 109 us
  Pallas kernels  107 us (97%)
  local copies, waits for them, and re-layouts  1.54 us (1%)
    pallas_call x1, Pallas kernels, layer(): pl.pallas_call(layer_kernel, out_shape=jax.ShapeDtypeStruct((TOK, PART),...  107 us

profile of v6, /device:TPU:2, one launch (start us, length us, event | category | flops | bytes accessed | tf_op | source)
XLA Modules:
  0.0 108.6 jit_solution(13861787863096918239)
XLA Ops:
  0.0 107.0 %layer.1 = bf16[128,384]{1,0:T(8,128)(2,1)} custom-call(bf16[128,1024]{1,0:T(8,128)(2,1)} %q_hbm.1, bf16[128,1024]{1,0:T(8,128)(2,1)} %k_hbm.1, bf16[128,1024]{1,0:T(8,128)(2,1)} %v_hbm.1, f32[8,128]{1,0:T(8,128)} %bitcast.19, s32[1,128]{1,0:T(1,128)} %bitcast.23, f32[1,1024]{1,0:T(1,128)} %bitcast.20, bf16[96,1024]{1,0:T(8,128)(2,1)} %bitcast.17, ...), custom_call_target="tpu_custom_call" | custom-call | tf_op jit(solution)/shard_map/layer/pallas_call | solution.py:701
  107.0 1.5 %copy.16 = bf16[128,384]{1,0:T(8,128)(2,1)} copy(bf16[128,384]{1,0:T(8,128)(2,1)} %layer.1) | data formatting | bytes 196608
